TPU v7x, 512 devices: a whole 4x4x16 slice. The times are simulated.
512 devices in a mesh: lon: 32 (over z, core), lat: 16 (over y, x).
Axes of the slice: x: 4, y: 4, z: 16, core: 2. Of those that a mesh axis runs over, the one named last changes fastest.
Arguments:
- perturbations: float32 [12, 3, 256, 4096], P(None, None, 'lat', 'lon'), as said below
- base_wind: float32 [2, 256, 4096], P(None, 'lat', 'lon'), may hold values from -4 to 4
- base_height: float32 [256, 4096], P('lat', 'lon'), may hold values from 0.5 to 1.5
Outputs:
- fields: float32 [12, 3, 256, 4096], P(None, None, 'lat', 'lon')
- factor: float32 [12, 12], replicated
Inputs may be any that keep to these rules, and one draw needn't show every extreme that they name: `perturbations`: finite real values.
All inputs are finite; a program needn't handle non-finite values.
Results may differ from a plain program's by a relative error of at most 0.00012.
Values sent between devices are 32-bit elements; how exact they have to be, the bound alone decides.
A program may use at most 64 MiB of HBM per device.

v0:
```python
import math

import jax
import jax.numpy as jnp
from jax import lax
from jax.sharding import PartitionSpec as P

STEPS = 8


advect_rate = 0.1
turn_rate = 0.5
gravity_rate = 0.2
diffuse_rate = 0.12


def with_halo(block, sides, width, periodic):
    for axis, dim in sides:
        count = lax.axis_size(axis)
        forward = [(i, i + 1) for i in range(count - 1)]
        if periodic:
            forward.append((count - 1, 0))
        backward = [(target, source) for source, target in forward]
        low = lax.ppermute(
            lax.slice_in_dim(block, block.shape[dim] - width, None, axis=dim), axis, forward
        )
        high = lax.ppermute(lax.slice_in_dim(block, 0, width, axis=dim), axis, backward)
        block = jnp.concatenate([low, block, high], axis=dim)
    return block


def centre(array):
    return array[..., 1:-1, 1:-1]


def diff_lon(array):
    return 0.5 * (array[..., 1:-1, 2:] - array[..., 1:-1, :-2])


def diff_lat(array):
    return 0.5 * (array[..., 2:, 1:-1] - array[..., :-2, 1:-1])


def laplacian(array):
    return (
        array[..., 2:, 1:-1]
        + array[..., :-2, 1:-1]
        + array[..., 1:-1, 2:]
        + array[..., 1:-1, :-2]
        - 4.0 * centre(array)
    )


def advance(field, base, turning):
    wind_x = field[..., 0, :, :]
    wind_y = field[..., 1, :, :]
    height = field[..., 2, :, :]
    base_x = base[0]
    base_y = base[1]
    base_depth = base[2]
    mean_x = centre(base_x)
    mean_y = centre(base_y)
    inner_x = centre(wind_x)
    inner_y = centre(wind_y)
    new_x = (
        inner_x
        - advect_rate
        * (
            mean_x * diff_lon(wind_x)
            + inner_x * diff_lon(base_x)
            + mean_y * diff_lat(wind_x)
            + inner_y * diff_lat(base_x)
        )
        + turn_rate * turning * inner_y
        - gravity_rate * diff_lon(height)
        + diffuse_rate * laplacian(wind_x)
    )
    new_y = (
        inner_y
        - advect_rate
        * (
            mean_x * diff_lon(wind_y)
            + inner_x * diff_lon(base_y)
            + mean_y * diff_lat(wind_y)
            + inner_y * diff_lat(base_y)
        )
        - turn_rate * turning * inner_x
        - gravity_rate * diff_lat(height)
        + diffuse_rate * laplacian(wind_y)
    )
    new_height = (
        centre(height)
        - advect_rate
        * (
            diff_lon(base_depth * wind_x + height * base_x)
            + diff_lat(base_depth * wind_y + height * base_y)
        )
        + diffuse_rate * laplacian(height)
    )
    return jnp.stack([new_x, new_y, new_height], axis=-3)


def coriolis(start, rows, total):
    glob = (start + jnp.arange(rows, dtype=jnp.int32)).astype(jnp.float32)
    return jnp.sin(math.pi * ((glob + 0.5) / total - 0.5))[:, None]


def inside_grid(start, rows, total):
    glob = start + jnp.arange(rows, dtype=jnp.int32)
    return ((glob >= 0) & (glob < total)).astype(jnp.float32)[:, None]


def extend(block, width):
    wide = with_halo(block, (("lon", 3),), width, True)
    return with_halo(wide, (("lat", 2),), width, False)


def per_device(perturbations, base_wind, base_height):
    rows = perturbations.shape[2]
    cols = perturbations.shape[3]
    total_rows = rows * lax.axis_size("lat")
    total_cols = cols * lax.axis_size("lon")
    row_start = lax.axis_index("lat") * rows
    depth = 2
    stacked = jnp.concatenate([base_wind, base_height[None]], axis=0)[None]
    base_ext = extend(stacked, depth)[0]
    field = perturbations
    for group_index in range(STEPS // depth):
        current = extend(field, depth)
        for inner_index in range(depth):
            margin = depth - 1 - inner_index
            turning = coriolis(row_start - margin, rows + 2 * margin, total_rows)
            base_margin = margin + 1
            current = advance(
                current,
                base_ext[
                    :,
                    depth - base_margin : depth + rows + base_margin,
                    depth - base_margin : depth + cols + base_margin,
                ],
                turning,
            )
            if margin > 0:
                current = current * inside_grid(row_start - margin, rows + 2 * margin, total_rows)
        field = current
    flattened = field.reshape(field.shape[0], -1)
    cell_count = float(3 * total_rows * total_cols)
    local_gram = jnp.dot(flattened, flattened.T, precision=lax.Precision.HIGHEST) / cell_count
    gram = lax.psum(local_gram, ("lon", "lat"))
    upper_factor = jnp.linalg.cholesky(gram).T
    lower_factor = upper_factor.T
    fields = jax.scipy.linalg.solve_triangular(lower_factor, flattened, lower=True)
    return (fields.reshape(perturbations.shape), upper_factor)


def solution(mesh):
    return jax.shard_map(
        per_device,
        mesh=mesh,
        in_specs=(P(None, None, "lat", "lon"), P(None, "lat", "lon"), P("lat", "lon")),
        out_specs=(P(None, None, "lat", "lon"), P()),
        check_vma=False,
    )
```

profile of v0, /device:TPU:1, one launch (start us, length us, event | category | flops | bytes accessed | tf_op | source)
XLA Modules:
  0.0 219.9 jit_solution(700765798616330664)
XLA Ops:
  0.6 0.7 maximum_bitcast_fusion
  1.4 3.0 %collective-permute-start.4 = (f32[1,3,16,2]{3,2,1,0:T(8,128)S(1)}, f32[1,3,16,2]{3,2,1,0:T(8,128)S(1)}, u32[]{:S(2)}, u32[]{:S(2)}) collective-permute-start(f32[1,3,16,2]{3,2,1,0:T(8,128)S(1)} %get-tuple-element.82), channel_id=1, source_target_pairs={{0,16},{16,32},{32,48},{48,64},{64,80},{80,96},{96,112},{112,128},... | collective-permute-start | bytes 1160 | tf_op jit(solution)/shard_map/ppermute | solution.py:24
  4.5 3.8 %collective-permute-start.5 = (f32[1,3,16,2]{3,2,1,0:T(8,128)S(1)}, f32[1,3,16,2]{3,2,1,0:T(8,128)S(1)}, u32[]{:S(2)}, u32[]{:S(2)}) collective-permute-start(f32[1,3,16,2]{3,2,1,0:T(8,128)S(1)} %get-tuple-element.83), channel_id=1, source_target_pairs={{16,0},{32,16},{48,32},{64,48},{80,64},{96,80},{112,96},{128,112},... | collective-permute-start | bytes 1160 | tf_op jit(solution)/shard_map/ppermute | solution.py:27
  8.3 1.1 copy.13
  9.6 3.6 %collective-permute-start.1 = (f32[12,3,16,2]{3,0,2,1:T(8,128)S(1)}, f32[12,3,16,2]{3,0,2,1:T(8,128)S(1)}, u32[]{:S(2)}, u32[]{:S(2)}) collective-permute-start(f32[12,3,16,2]{3,0,2,1:T(8,128)S(1)} %get-tuple-element.61), channel_id=1, source_target_pairs={{16,0},{32,16},{48,32},{64,48},{80,64},{96,80},{112,96},{128,112},... | collective-permute-start | bytes 13832 | tf_op jit(solution)/shard_map/ppermute | solution.py:27
  13.3 3.1 %collective-permute-start.6 = (f32[1,3,2,132]{3,2,1,0:T(2,128)S(1)}, f32[1,3,2,132]{3,2,1,0:T(2,128)S(1)}, u32[]{:S(2)}, u32[]{:S(2)}) collective-permute-start(f32[1,3,2,132]{3,2,1,0:T(2,128)S(1)} %get-tuple-element.68), channel_id=1, source_target_pairs={{0,1},{1,2},{2,3},{3,4},{4,5},{5,6},{6,7},{7,8},{8,9},{9,10},{10,1... | collective-permute-start | bytes 9512 | tf_op jit(solution)/shard_map/ppermute | solution.py:24
  16.5 1.3 collective-permute-start.7
  17.8 3.3 %collective-permute-done.7 = f32[1,3,2,132]{3,2,1,0:T(2,128)S(1)} collective-permute-done((f32[1,3,2,132]{3,2,1,0:T(2,128)S(1)}, f32[1,3,2,132]{3,2,1,0:T(2,128)S(1)}, u32[]{:S(2)}, u32[]{:S(2)}) %collective-permute-start.7) | collective-permute-done | bytes 3200 | tf_op jit(solution)/shard_map/ppermute | solution.py:27
  21.7 3.1 %collective-permute-start.2 = (f32[12,3,2,132]{3,0,2,1:T(8,128)S(1)}, f32[12,3,2,132]{3,0,2,1:T(8,128)S(1)}, u32[]{:S(2)}, u32[]{:S(2)}) collective-permute-start(f32[12,3,2,132]{3,0,2,1:T(8,128)S(1)} %get-tuple-element.12), channel_id=1, source_target_pairs={{0,1},{1,2},{2,3},{3,4},{4,5},{5,6},{6,7},{7,8},{8,9},{9,10},{10,1... | collective-permute-start | bytes 114056 | tf_op jit(solution)/shard_map/ppermute | solution.py:24
  24.9 1.3 collective-permute-start.3
  26.5 3.7 %collective-permute-done.3 = f32[12,3,2,132]{3,0,2,1:T(8,128)S(1)} collective-permute-done((f32[12,3,2,132]{3,0,2,1:T(8,128)S(1)}, f32[12,3,2,132]{3,0,2,1:T(8,128)S(1)}, u32[]{:S(2)}, u32[]{:S(2)}) %collective-permute-start.3) | collective-permute-done | bytes 38048 | tf_op jit(solution)/shard_map/ppermute | solution.py:27
  30.2 0.4 pad_maximum_fusion
  30.8 0.6 add_bitcast_fusion.7
  31.4 0.6 add_bitcast_fusion.6
  32.0 0.6 fusion.22
  33.3 0.3 add_bitcast_fusion.14
  33.6 0.3 fusion.42
  34.2 5.5 %collective-permute-start.9 = (f32[12,3,16,2]{3,0,2,1:T(8,128)S(1)}, f32[12,3,16,2]{3,0,2,1:T(8,128)S(1)}, u32[]{:S(2)}, u32[]{:S(2)}) collective-permute-start(f32[12,3,16,2]{3,0,2,1:T(8,128)S(1)} %get-tuple-element.59), channel_id=1, source_target_pairs={{16,0},{32,16},{48,32},{64,48},{80,64},{96,80},{112,96},{128,112},... | collective-permute-start | bytes 13832 | tf_op jit(solution)/shard_map/ppermute | solution.py:27
  39.7 1.2 collective-permute-done.8
  40.9 0.5 collective-permute-done.9
  41.5 4.7 %collective-permute-start.10 = (f32[12,3,2,132]{3,0,2,1:T(8,128)S(1)}, f32[12,3,2,132]{3,0,2,1:T(8,128)S(1)}, u32[]{:S(2)}, u32[]{:S(2)}) collective-permute-start(f32[12,3,2,132]{3,0,2,1:T(8,128)S(1)} %get-tuple-element.10), channel_id=1, source_target_pairs={{0,1},{1,2},{2,3},{3,4},{4,5},{5,6},{6,7},{7,8},{8,9},{9,10},{10,1... | collective-permute-start | bytes 114056 | tf_op jit(solution)/shard_map/ppermute | solution.py:24
  46.2 1.3 collective-permute-start.11
  47.5 0.3 collective-permute-done.10
  47.8 3.7 %collective-permute-done.11 = f32[12,3,2,132]{3,0,2,1:T(8,128)S(1)} collective-permute-done((f32[12,3,2,132]{3,0,2,1:T(8,128)S(1)}, f32[12,3,2,132]{3,0,2,1:T(8,128)S(1)}, u32[]{:S(2)}, u32[]{:S(2)}) %collective-permute-start.11) | collective-permute-done | bytes 38048 | tf_op jit(solution)/shard_map/ppermute | solution.py:27
  51.6 0.4 pad_maximum_fusion.1
  52.0 0.6 add_bitcast_fusion.5
  52.6 0.6 add_bitcast_fusion.4
  53.4 0.6 fusion.17
  54.5 0.3 add_bitcast_fusion.12
  55.0 0.3 fusion.37
  55.5 1.9 collective-permute-start.12
  57.4 6.0 %collective-permute-start.13 = (f32[12,3,16,2]{3,0,2,1:T(8,128)S(1)}, f32[12,3,16,2]{3,0,2,1:T(8,128)S(1)}, u32[]{:S(2)}, u32[]{:S(2)}) collective-permute-start(f32[12,3,16,2]{3,0,2,1:T(8,128)S(1)} %get-tuple-element.57), channel_id=1, source_target_pairs={{16,0},{32,16},{48,32},{64,48},{80,64},{96,80},{112,96},{128,112},... | collective-permute-start | bytes 13832 | tf_op jit(solution)/shard_map/ppermute | solution.py:27
  63.4 1.2 collective-permute-done.12
  64.9 3.8 %collective-permute-start.14 = (f32[12,3,2,132]{3,0,2,1:T(8,128)S(1)}, f32[12,3,2,132]{3,0,2,1:T(8,128)S(1)}, u32[]{:S(2)}, u32[]{:S(2)}) collective-permute-start(f32[12,3,2,132]{3,0,2,1:T(8,128)S(1)} %get-tuple-element.8), channel_id=1, source_target_pairs={{0,1},{1,2},{2,3},{3,4},{4,5},{5,6},{6,7},{7,8},{8,9},{9,10},{10,1... | collective-permute-start | bytes 114056 | tf_op jit(solution)/shard_map/ppermute | solution.py:24
  68.6 1.5 collective-permute-start.15
  70.2 4.0 %collective-permute-done.15 = f32[12,3,2,132]{3,0,2,1:T(8,128)S(1)} collective-permute-done((f32[12,3,2,132]{3,0,2,1:T(8,128)S(1)}, f32[12,3,2,132]{3,0,2,1:T(8,128)S(1)}, u32[]{:S(2)}, u32[]{:S(2)}) %collective-permute-start.15) | collective-permute-done | bytes 38048 | tf_op jit(solution)/shard_map/ppermute | solution.py:27
  74.3 0.4 pad_maximum_fusion.2
  74.7 0.6 add_bitcast_fusion.3
  75.3 0.6 add_bitcast_fusion.2
  76.1 0.6 fusion.12
  77.2 0.3 add_bitcast_fusion.10
  77.6 0.3 fusion.32
  78.2 1.0 collective-permute-start.16
  79.2 7.2 %collective-permute-start.17 = (f32[12,3,16,2]{3,0,2,1:T(8,128)S(1)}, f32[12,3,16,2]{3,0,2,1:T(8,128)S(1)}, u32[]{:S(2)}, u32[]{:S(2)}) collective-permute-start(f32[12,3,16,2]{3,0,2,1:T(8,128)S(1)} %get-tuple-element.55), channel_id=1, source_target_pairs={{16,0},{32,16},{48,32},{64,48},{80,64},{96,80},{112,96},{128,112},... | collective-permute-start | bytes 13832 | tf_op jit(solution)/shard_map/ppermute | solution.py:27
  86.4 1.2 collective-permute-done.16
  87.9 3.8 %collective-permute-start.18 = (f32[12,3,2,132]{3,0,2,1:T(8,128)S(1)}, f32[12,3,2,132]{3,0,2,1:T(8,128)S(1)}, u32[]{:S(2)}, u32[]{:S(2)}) collective-permute-start(f32[12,3,2,132]{3,0,2,1:T(8,128)S(1)} %get-tuple-element.6), channel_id=1, source_target_pairs={{0,1},{1,2},{2,3},{3,4},{4,5},{5,6},{6,7},{7,8},{8,9},{9,10},{10,1... | collective-permute-start | bytes 114056 | tf_op jit(solution)/shard_map/ppermute | solution.py:24
  91.7 1.3 collective-permute-start.19
  93.0 0.3 collective-permute-done.18
  93.3 4.0 %collective-permute-done.19 = f32[12,3,2,132]{3,0,2,1:T(8,128)S(1)} collective-permute-done((f32[12,3,2,132]{3,0,2,1:T(8,128)S(1)}, f32[12,3,2,132]{3,0,2,1:T(8,128)S(1)}, u32[]{:S(2)}, u32[]{:S(2)}) %collective-permute-start.19) | collective-permute-done | bytes 38048 | tf_op jit(solution)/shard_map/ppermute | solution.py:27
  97.3 0.4 pad_maximum_fusion.3
  97.7 0.6 add_bitcast_fusion.1
  98.3 0.6 add_bitcast_fusion
  99.1 0.6 fusion.7
  100.2 0.3 add_bitcast_fusion.8
  100.7 0.3 fusion.27
  101.0 0.6 fusion
  101.7 112.7 %psum.7 = f32[12,12]{0,1:T(8,128)S(1)} all-reduce(f32[12,12]{0,1:T(8,128)S(1)} %fusion), channel_id=1, replica_groups=mesh['lon'=32,'lat'=16] {'lon','lat'}, use_global_device_ids=true, to_apply=%region_0.0 | all-reduce | flops 144 | bytes 1152 | tf_op jit(solution)/shard_map/psum | solution.py:149
  214.4 1.1 cholesky.16
  215.5 0.6 compare_reduce_fusion
  216.2 0.6 fusion.53
  216.9 0.9 custom-call.7
  217.9 0.5 fusion.1
  218.4 0.8 copy.21
  219.2 0.7 copy.22
  (62 shorter events, 6.4 us)
Async XLA Ops:
  1.4 11.8 %collective-permute-start.4 = (f32[1,3,16,2]{3,2,1,0:T(8,128)S(1)}, f32[1,3,16,2]{3,2,1,0:T(8,128)S(1)}, u32[]{:S(2)}, u32[]{:S(2)}) collective-permute-start(f32[1,3,16,2]{3,2,1,0:T(8,128)S(1)} %get-tuple-element.82), channel_id=1, source_target_pairs={{0,16},{16,32},{32,48},{48,64},{64,80},{80,96},{96,112},{112,128},... | collective-permute-start | bytes 1160 | tf_op jit(solution)/shard_map/ppermute | solution.py:24
  4.5 8.8 %collective-permute-start.5 = (f32[1,3,16,2]{3,2,1,0:T(8,128)S(1)}, f32[1,3,16,2]{3,2,1,0:T(8,128)S(1)}, u32[]{:S(2)}, u32[]{:S(2)}) collective-permute-start(f32[1,3,16,2]{3,2,1,0:T(8,128)S(1)} %get-tuple-element.83), channel_id=1, source_target_pairs={{16,0},{32,16},{48,32},{64,48},{80,64},{96,80},{112,96},{128,112},... | collective-permute-start | bytes 1160 | tf_op jit(solution)/shard_map/ppermute | solution.py:27
  9.5 12.0 %collective-permute-start = (f32[12,3,16,2]{3,0,2,1:T(8,128)S(1)}, f32[12,3,16,2]{3,0,2,1:T(8,128)S(1)}, u32[]{:S(2)}, u32[]{:S(2)}) collective-permute-start(f32[12,3,16,2]{3,0,2,1:T(8,128)S(1)} %get-tuple-element.60), channel_id=1, source_target_pairs={{0,16},{16,32},{32,48},{48,64},{64,80},{80,96},{96,112},{112,128},... | collective-permute-start | bytes 13832 | tf_op jit(solution)/shard_map/ppermute | solution.py:24
  9.6 12.0 %collective-permute-start.1 = (f32[12,3,16,2]{3,0,2,1:T(8,128)S(1)}, f32[12,3,16,2]{3,0,2,1:T(8,128)S(1)}, u32[]{:S(2)}, u32[]{:S(2)}) collective-permute-start(f32[12,3,16,2]{3,0,2,1:T(8,128)S(1)} %get-tuple-element.61), channel_id=1, source_target_pairs={{16,0},{32,16},{48,32},{64,48},{80,64},{96,80},{112,96},{128,112},... | collective-permute-start | bytes 13832 | tf_op jit(solution)/shard_map/ppermute | solution.py:27
  13.3 4.5 %collective-permute-start.6 = (f32[1,3,2,132]{3,2,1,0:T(2,128)S(1)}, f32[1,3,2,132]{3,2,1,0:T(2,128)S(1)}, u32[]{:S(2)}, u32[]{:S(2)}) collective-permute-start(f32[1,3,2,132]{3,2,1,0:T(2,128)S(1)} %get-tuple-element.68), channel_id=1, source_target_pairs={{0,1},{1,2},{2,3},{3,4},{4,5},{5,6},{6,7},{7,8},{8,9},{9,10},{10,1... | collective-permute-start | bytes 9512 | tf_op jit(solution)/shard_map/ppermute | solution.py:24
  16.5 4.7 %collective-permute-start.7 = (f32[1,3,2,132]{3,2,1,0:T(2,128)S(1)}, f32[1,3,2,132]{3,2,1,0:T(2,128)S(1)}, u32[]{:S(2)}, u32[]{:S(2)}) collective-permute-start(f32[1,3,2,132]{3,2,1,0:T(2,128)S(1)} %get-tuple-element.69), channel_id=1, source_target_pairs={{1,0},{2,1},{3,2},{4,3},{5,4},{6,5},{7,6},{8,7},{9,8},{10,9},{11,1... | collective-permute-start | bytes 9512 | tf_op jit(solution)/shard_map/ppermute | solution.py:27
  21.7 4.7 %collective-permute-start.2 = (f32[12,3,2,132]{3,0,2,1:T(8,128)S(1)}, f32[12,3,2,132]{3,0,2,1:T(8,128)S(1)}, u32[]{:S(2)}, u32[]{:S(2)}) collective-permute-start(f32[12,3,2,132]{3,0,2,1:T(8,128)S(1)} %get-tuple-element.12), channel_id=1, source_target_pairs={{0,1},{1,2},{2,3},{3,4},{4,5},{5,6},{6,7},{7,8},{8,9},{9,10},{10,1... | collective-permute-start | bytes 114056 | tf_op jit(solution)/shard_map/ppermute | solution.py:24
  24.9 5.4 %collective-permute-start.3 = (f32[12,3,2,132]{3,0,2,1:T(8,128)S(1)}, f32[12,3,2,132]{3,0,2,1:T(8,128)S(1)}, u32[]{:S(2)}, u32[]{:S(2)}) collective-permute-start(f32[12,3,2,132]{3,0,2,1:T(8,128)S(1)} %get-tuple-element.13), channel_id=1, source_target_pairs={{1,0},{2,1},{3,2},{4,3},{5,4},{6,5},{7,6},{8,7},{9,8},{10,9},{11,1... | collective-permute-start | bytes 114056 | tf_op jit(solution)/shard_map/ppermute | solution.py:27
  34.1 6.7 %collective-permute-start.8 = (f32[12,3,16,2]{3,0,2,1:T(8,128)S(1)}, f32[12,3,16,2]{3,0,2,1:T(8,128)S(1)}, u32[]{:S(2)}, u32[]{:S(2)}) collective-permute-start(f32[12,3,16,2]{3,0,2,1:T(8,128)S(1)} %get-tuple-element.58), channel_id=1, source_target_pairs={{0,16},{16,32},{32,48},{48,64},{64,80},{80,96},{96,112},{112,128},... | collective-permute-start | bytes 13832 | tf_op jit(solution)/shard_map/ppermute | solution.py:24
  34.2 7.2 %collective-permute-start.9 = (f32[12,3,16,2]{3,0,2,1:T(8,128)S(1)}, f32[12,3,16,2]{3,0,2,1:T(8,128)S(1)}, u32[]{:S(2)}, u32[]{:S(2)}) collective-permute-start(f32[12,3,16,2]{3,0,2,1:T(8,128)S(1)} %get-tuple-element.59), channel_id=1, source_target_pairs={{16,0},{32,16},{48,32},{64,48},{80,64},{96,80},{112,96},{128,112},... | collective-permute-start | bytes 13832 | tf_op jit(solution)/shard_map/ppermute | solution.py:27
  41.5 6.3 %collective-permute-start.10 = (f32[12,3,2,132]{3,0,2,1:T(8,128)S(1)}, f32[12,3,2,132]{3,0,2,1:T(8,128)S(1)}, u32[]{:S(2)}, u32[]{:S(2)}) collective-permute-start(f32[12,3,2,132]{3,0,2,1:T(8,128)S(1)} %get-tuple-element.10), channel_id=1, source_target_pairs={{0,1},{1,2},{2,3},{3,4},{4,5},{5,6},{6,7},{7,8},{8,9},{9,10},{10,1... | collective-permute-start | bytes 114056 | tf_op jit(solution)/shard_map/ppermute | solution.py:24
  46.2 5.4 %collective-permute-start.11 = (f32[12,3,2,132]{3,0,2,1:T(8,128)S(1)}, f32[12,3,2,132]{3,0,2,1:T(8,128)S(1)}, u32[]{:S(2)}, u32[]{:S(2)}) collective-permute-start(f32[12,3,2,132]{3,0,2,1:T(8,128)S(1)} %get-tuple-element.11), channel_id=1, source_target_pairs={{1,0},{2,1},{3,2},{4,3},{5,4},{6,5},{7,6},{8,7},{9,8},{10,9},{11,1... | collective-permute-start | bytes 114056 | tf_op jit(solution)/shard_map/ppermute | solution.py:27
  55.5 9.1 %collective-permute-start.12 = (f32[12,3,16,2]{3,0,2,1:T(8,128)S(1)}, f32[12,3,16,2]{3,0,2,1:T(8,128)S(1)}, u32[]{:S(2)}, u32[]{:S(2)}) collective-permute-start(f32[12,3,16,2]{3,0,2,1:T(8,128)S(1)} %get-tuple-element.56), channel_id=1, source_target_pairs={{0,16},{16,32},{32,48},{48,64},{64,80},{80,96},{96,112},{112,128},... | collective-permute-start | bytes 13832 | tf_op jit(solution)/shard_map/ppermute | solution.py:24
  57.4 7.4 %collective-permute-start.13 = (f32[12,3,16,2]{3,0,2,1:T(8,128)S(1)}, f32[12,3,16,2]{3,0,2,1:T(8,128)S(1)}, u32[]{:S(2)}, u32[]{:S(2)}) collective-permute-start(f32[12,3,16,2]{3,0,2,1:T(8,128)S(1)} %get-tuple-element.57), channel_id=1, source_target_pairs={{16,0},{32,16},{48,32},{64,48},{80,64},{96,80},{112,96},{128,112},... | collective-permute-start | bytes 13832 | tf_op jit(solution)/shard_map/ppermute | solution.py:27
  64.9 5.4 %collective-permute-start.14 = (f32[12,3,2,132]{3,0,2,1:T(8,128)S(1)}, f32[12,3,2,132]{3,0,2,1:T(8,128)S(1)}, u32[]{:S(2)}, u32[]{:S(2)}) collective-permute-start(f32[12,3,2,132]{3,0,2,1:T(8,128)S(1)} %get-tuple-element.8), channel_id=1, source_target_pairs={{0,1},{1,2},{2,3},{3,4},{4,5},{5,6},{6,7},{7,8},{8,9},{9,10},{10,1... | collective-permute-start | bytes 114056 | tf_op jit(solution)/shard_map/ppermute | solution.py:24
  68.6 5.6 %collective-permute-start.15 = (f32[12,3,2,132]{3,0,2,1:T(8,128)S(1)}, f32[12,3,2,132]{3,0,2,1:T(8,128)S(1)}, u32[]{:S(2)}, u32[]{:S(2)}) collective-permute-start(f32[12,3,2,132]{3,0,2,1:T(8,128)S(1)} %get-tuple-element.9), channel_id=1, source_target_pairs={{1,0},{2,1},{3,2},{4,3},{5,4},{6,5},{7,6},{8,7},{9,8},{10,9},{11,1... | collective-permute-start | bytes 114056 | tf_op jit(solution)/shard_map/ppermute | solution.py:27
  78.2 9.4 %collective-permute-start.16 = (f32[12,3,16,2]{3,0,2,1:T(8,128)S(1)}, f32[12,3,16,2]{3,0,2,1:T(8,128)S(1)}, u32[]{:S(2)}, u32[]{:S(2)}) collective-permute-start(f32[12,3,16,2]{3,0,2,1:T(8,128)S(1)} %get-tuple-element.54), channel_id=1, source_target_pairs={{0,16},{16,32},{32,48},{48,64},{64,80},{80,96},{96,112},{112,128},... | collective-permute-start | bytes 13832 | tf_op jit(solution)/shard_map/ppermute | solution.py:24
  79.2 8.6 %collective-permute-start.17 = (f32[12,3,16,2]{3,0,2,1:T(8,128)S(1)}, f32[12,3,16,2]{3,0,2,1:T(8,128)S(1)}, u32[]{:S(2)}, u32[]{:S(2)}) collective-permute-start(f32[12,3,16,2]{3,0,2,1:T(8,128)S(1)} %get-tuple-element.55), channel_id=1, source_target_pairs={{16,0},{32,16},{48,32},{64,48},{80,64},{96,80},{112,96},{128,112},... | collective-permute-start | bytes 13832 | tf_op jit(solution)/shard_map/ppermute | solution.py:27
  87.9 5.4 %collective-permute-start.18 = (f32[12,3,2,132]{3,0,2,1:T(8,128)S(1)}, f32[12,3,2,132]{3,0,2,1:T(8,128)S(1)}, u32[]{:S(2)}, u32[]{:S(2)}) collective-permute-start(f32[12,3,2,132]{3,0,2,1:T(8,128)S(1)} %get-tuple-element.6), channel_id=1, source_target_pairs={{0,1},{1,2},{2,3},{3,4},{4,5},{5,6},{6,7},{7,8},{8,9},{9,10},{10,1... | collective-permute-start | bytes 114056 | tf_op jit(solution)/shard_map/ppermute | solution.py:24
  91.7 5.6 %collective-permute-start.19 = (f32[12,3,2,132]{3,0,2,1:T(8,128)S(1)}, f32[12,3,2,132]{3,0,2,1:T(8,128)S(1)}, u32[]{:S(2)}, u32[]{:S(2)}) collective-permute-start(f32[12,3,2,132]{3,0,2,1:T(8,128)S(1)} %get-tuple-element.7), channel_id=1, source_target_pairs={{1,0},{2,1},{3,2},{4,3},{5,4},{6,5},{7,6},{8,7},{9,8},{10,9},{11,1... | collective-permute-start | bytes 114056 | tf_op jit(solution)/shard_map/ppermute | solution.py:27
where the time goes:
time: 221 us; the launch traced here: 220 us
  blocking collectives  113 us (51%)
  starting transfers between devices  57.2 us (26%)
  waiting for transfers between devices  24.3 us (11%)
  other arithmetic  19.3 us (9%)
  local copies, waits for them, and re-layouts  4.13 us (2%)
    psum x1, blocking collectives, per_device(): gram = lax.psum(local_gram, ('lon', 'lat'))  113 us
    ppermute x10, starting transfers between devices, with_halo(): lax.ppermute(lax.slice_in_dim(block, 0, width, axis=dim), axis, backward)  32.8 us
    ppermute x10, starting transfers between devices, with_halo(): lax.ppermute(lax.slice_in_dim(block, block.shape[dim] - width, None, axis...  24.4 us
    ppermute x10, waiting for transfers between devices, with_halo(): lax.ppermute(lax.slice_in_dim(block, 0, width, axis=dim), axis, backward)  19.7 us
    another operation x28, other arithmetic, advance(): return jnp.stack([new_x, new_y, new_height], axis=-3)  11 us
    ppermute x10, waiting for transfers between devices, with_halo(): lax.ppermute(lax.slice_in_dim(block, block.shape[dim] - width, None, axis...  4.58 us
  transfers between devices with their start and end apart: 20, of which 15 were waited for; matrix products, arithmetic and copies ran while one was open for 1% of the time, Pallas kernels for 0%

commit v1 on v0

v1 whole, which is shorter than its diff:
```python
import functools
import math

import jax
import jax.numpy as jnp
from jax import lax
from jax.experimental import pallas as pl
from jax.experimental.pallas import tpu as pltpu
from jax.sharding import PartitionSpec as P

MEMBERS = 12
STEPS = 8
GROUP = 4
GROUPS = MEMBERS // GROUP
WIDTH = 8
EDGE = 24
STRIP = 32

advect_rate = 0.1
turn_rate = 0.5
gravity_rate = 0.2
diffuse_rate = 0.12

HALF = 0.5 * advect_rate
KEEP = 1.0 - 4.0 * diffuse_rate
PULL = 0.5 * gravity_rate
COEFS = 13


def roll(value, shift):
    shift = shift % 128
    return value if shift == 0 else pltpu.roll(value, shift, 1)


def lanes_of(rows):
    return lax.broadcasted_iota(jnp.int32, (rows, 128), 1)


def rows_of(rows):
    return lax.broadcasted_iota(jnp.int32, (rows, 128), 0)


def slot_of(local, var):
    return WIDTH * (3 * local + var)


def kernel(
    n_lon,
    n_lat,
    x_hbm,
    wind_hbm,
    height_hbm,
    fields_ref,
    factor_ref,
    ext,
    send_low,
    send_high,
    from_west,
    from_east,
    flow,
    base,
    coef,
    evolved,
    table,
    row_out,
    plane_in,
    column_in,
    load_sem,
    lat_send,
    lat_recv,
    strip_send,
    strip_recv,
    plane_send,
    plane_recv,
    column_send,
    column_recv,
):
    lon = lax.axis_index("lon")
    lat = lax.axis_index("lat")
    level = lon // 2
    core = lon % 2
    n_level = n_lon // 2
    n_plane = 2 * n_lat
    me_plane = lat * 2 + core
    east = (lon + 1) % n_lon
    west = (lon + n_lon - 1) % n_lon
    has_south = lat > 0
    has_north = lat < n_lat - 1

    def device(lon_index, lat_index):
        return {"lon": lon_index, "lat": lat_index}

    loads = [
        pltpu.make_async_copy(x_hbm, ext.at[0:MEMBERS, :, 8:24], load_sem.at[0]),
        pltpu.make_async_copy(wind_hbm, ext.at[MEMBERS, 0:2, 8:24], load_sem.at[1]),
        pltpu.make_async_copy(height_hbm, ext.at[MEMBERS, 2, 8:24], load_sem.at[2]),
    ]
    for load in loads:
        load.start()

    def plane_peer(step):
        index = (me_plane + step) % n_plane
        return device(level * 2 + index % 2, index // 2)

    def column_peer(step):
        return device(((level + step) % n_level) * 2 + core, lat)

    barrier = pltpu.get_barrier_semaphore()
    across = jnp.where(core == 1, east, west)

    @pl.loop(1, n_plane)
    def _(step):
        pl.semaphore_signal(barrier, inc=1, device_id=plane_peer(step))

    @pl.loop(1, n_level)
    def _(step):
        pl.semaphore_signal(barrier, inc=1, device_id=column_peer(step))

    pl.semaphore_signal(barrier, inc=1, device_id=device(across, lat))

    @pl.when(has_south)
    def _():
        pl.semaphore_signal(barrier, inc=1, device_id=device(across, lat - 1))

    @pl.when(has_north)
    def _():
        pl.semaphore_signal(barrier, inc=1, device_id=device(across, lat + 1))

    def lat_copies(piece, north):
        rows = pl.ds(8, 8) if north else pl.ds(0, 8)
        place = pl.ds(0, 8) if north else pl.ds(24, 8)
        way = 0 if north else 1
        target = device(lon, lat + 1 if north else lat - 1)
        if piece == "wind":
            source, goal, sem = wind_hbm.at[:, rows], ext.at[MEMBERS, 0:2, place], GROUPS
        elif piece == "height":
            source, goal, sem = height_hbm.at[rows], ext.at[MEMBERS, 2, place], GROUPS + 1
        else:
            members = pl.ds(piece * GROUP, GROUP)
            source, goal, sem = x_hbm.at[members, :, rows], ext.at[members, :, place], piece
        return pltpu.make_async_remote_copy(
            src_ref=source,
            dst_ref=goal,
            send_sem=lat_send.at[way, sem],
            recv_sem=lat_recv.at[way, sem],
            device_id=target,
        )

    def strip_copy(to_east, shift):
        packed = send_high if to_east else send_low
        goal = from_west if to_east else from_east
        rows = {0: pl.ds(0, 16), 1: pl.ds(8, 8), -1: pl.ds(0, 8)}[shift]
        place = {0: pl.ds(8, 16), 1: pl.ds(0, 8), -1: pl.ds(24, 8)}[shift]
        sem = (0 if to_east else 3) + shift + 1
        return pltpu.make_async_remote_copy(
            src_ref=packed.at[:, rows],
            dst_ref=goal.at[:, place],
            send_sem=strip_send.at[sem],
            recv_sem=strip_recv.at[sem],
            device_id=device(east if to_east else west, lat + shift),
        )

    def when_sends(north, body):
        pl.when(has_north if north else has_south)(body)

    def when_receives(north, body):
        pl.when(has_south if north else has_north)(body)

    lane8 = lanes_of(8)

    for load in loads:
        load.wait()

    lane16 = lanes_of(16)

    @pl.loop(0, GROUPS)
    def _(group):
        low = jnp.zeros((16, 128), jnp.float32)
        high = jnp.zeros((16, 128), jnp.float32)
        for local in range(GROUP + 1):
            for var in range(3):
                value = ext[group * GROUP + local if local < GROUP else MEMBERS, var, pl.ds(8, 16)]
                slot = slot_of(local, var)
                inside = (lane16 >= slot) & (lane16 < slot + WIDTH)
                low = jnp.where(inside, roll(value, slot), low)
                high = jnp.where(inside, roll(value, slot - 120), high)
        send_low[group] = low
        send_high[group] = high

    pl.semaphore_wait(
        barrier,
        n_plane - 1 + n_level - 1 + 1 + has_south.astype(jnp.int32) + has_north.astype(jnp.int32),
    )

    for piece in ("wind", "height"):
        for north in (True, False):
            when_sends(north, lambda: lat_copies(piece, north).start())
    for to_east in (True, False):
        strip_copy(to_east, 0).start()
        pl.when(has_north)(lambda: strip_copy(to_east, 1).start())
        pl.when(has_south)(lambda: strip_copy(to_east, -1).start())
    for piece in range(GROUPS):
        for north in (True, False):
            when_sends(north, lambda: lat_copies(piece, north).start())

    evolved[MEMBERS * 48 :, :] = jnp.zeros((4 * 48, 128), jnp.float32)
    for parity in range(2):
        for slot in range(GROUP + 1):
            for var in range(3):
                flow[parity, slot, var, 0:8] = jnp.zeros((8, 128), jnp.float32)
                flow[parity, slot, var, 40:48] = jnp.zeros((8, 128), jnp.float32)
    for kind in range(2):
        for var in range(3):
            base[kind, var, 0:8] = jnp.zeros((8, 128), jnp.float32)
            base[kind, var, 40:48] = jnp.zeros((8, 128), jnp.float32)

    for piece in ("wind", "height"):
        for north in (True, False):
            when_receives(north, lambda: lat_copies(piece, north).wait_recv())
    for to_east in (True, False):
        strip_copy(to_east, 0).wait_recv()
        pl.when(has_south)(lambda: strip_copy(to_east, 1).wait_recv())
        pl.when(has_north)(lambda: strip_copy(to_east, -1).wait_recv())

    def present(tile, value):
        if tile == 0:
            return jnp.where(has_south, value, 0.0)
        if tile == 3:
            return jnp.where(has_north, value, 0.0)
        return value

    def shifted_main(group, member, local, var, tile):
        rows = pl.ds(8 * tile, 8)
        rim = roll(from_west[group, rows], -slot_of(local, var))
        return present(tile, jnp.where(lane8 < WIDTH, rim, roll(ext[member, var, rows], WIDTH)))

    def strip_part(total, group, member, local, var, place, tile):
        rows = pl.ds(8 * tile, 8)
        first = place * STRIP
        own = roll(ext[member, var, rows], first - (128 - EDGE))
        rim = roll(from_east[group, rows], first + EDGE - slot_of(local, var))
        total = jnp.where((lane8 >= first) & (lane8 < first + EDGE), own, total)
        return jnp.where((lane8 >= first + EDGE) & (lane8 < first + STRIP), rim, total)

    for var in range(3):
        for tile in range(4):
            rows = pl.ds(8 + 8 * tile, 8)
            base[0, var, rows] = shifted_main(0, MEMBERS, GROUP, var, tile)
            total = jnp.zeros((8, 128), jnp.float32)
            for place in range(4):
                total = strip_part(total, 0, MEMBERS, GROUP, var, place, tile)
            base[1, var, rows] = present(tile, total)
    for tile in range(4):
        place = (lat * 16 - 8 + 8 * tile + rows_of(8)).astype(jnp.float32)
        turning = jnp.sin(math.pi * ((place + 0.5) / (16 * n_lat) - 0.5))
        for kind in range(2):
            here, up, down = pl.ds(8 + 8 * tile, 8), pl.ds(9 + 8 * tile, 8), pl.ds(7 + 8 * tile, 8)
            mean_x = base[kind, 0, here]
            mean_y = base[kind, 1, here]
            depth = base[kind, 2, here]
            x_up, x_down = base[kind, 0, up], base[kind, 0, down]
            y_up, y_down = base[kind, 1, up], base[kind, 1, down]
            values = [
                diffuse_rate - HALF * mean_x,
                diffuse_rate + HALF * mean_x,
                diffuse_rate - HALF * mean_y,
                diffuse_rate + HALF * mean_y,
                KEEP - HALF * (roll(mean_x, -1) - roll(mean_x, 1)),
                turn_rate * turning - HALF * (x_up - x_down),
                KEEP - HALF * (y_up - y_down),
                -turn_rate * turning - HALF * (roll(mean_y, -1) - roll(mean_y, 1)),
                HALF * depth,
                diffuse_rate - HALF * y_up,
                diffuse_rate + HALF * y_down,
                HALF * base[kind, 2, up],
                HALF * base[kind, 2, down],
            ]
            for index, value in enumerate(values):
                coef[index, kind, pl.ds(8 * tile, 8)] = value

    def advance(source, target, tiles):
        for tile in tiles:
            here, up, down = pl.ds(8 + 8 * tile, 8), pl.ds(9 + 8 * tile, 8), pl.ds(7 + 8 * tile, 8)
            for kind, slots in ((0, range(GROUP)), (1, (GROUP,))):
                (e, w, n, s, keep_x, turn_x, keep_y, turn_y, deep, n_h, s_h, n_deep, s_deep) = [
                    coef[index, kind, pl.ds(8 * tile, 8)] for index in range(COEFS)
                ]
                for slot in slots:
                    u, u_n, u_s = (flow[source, slot, 0, r] for r in (here, up, down))
                    v, v_n, v_s = (flow[source, slot, 1, r] for r in (here, up, down))
                    h, h_n, h_s = (flow[source, slot, 2, r] for r in (here, up, down))
                    new_u = (
                        (keep_x * u + turn_x * v)
                        + (n * u_n + s * u_s)
                        + (e * roll(u, -1) + w * roll(u, 1))
                        - PULL * (roll(h, -1) - roll(h, 1))
                    )
                    new_v = (
                        (keep_y * v + turn_y * u)
                        + (n * v_n + s * v_s)
                        + (e * roll(v, -1) + w * roll(v, 1))
                        - PULL * (h_n - h_s)
                    )
                    carried = deep * u
                    new_h = (
                        KEEP * h
                        + (roll(e * h - carried, -1) + roll(w * h + carried, 1))
                        + (n_h * h_n + s_h * h_s)
                        - (n_deep * v_n - s_deep * v_s)
                    )
                    flow[target, slot, 0, here] = present(tile, new_u)
                    flow[target, slot, 1, here] = present(tile, new_v)
                    flow[target, slot, 2, here] = present(tile, new_h)

    @pl.loop(0, GROUPS)
    def _(group):
        for north in (True, False):
            when_receives(north, lambda: lat_copies(group, north).wait_recv())
        for var in range(3):
            for tile in range(4):
                rows = pl.ds(8 + 8 * tile, 8)
                total = jnp.zeros((8, 128), jnp.float32)
                for local in range(GROUP):
                    member = group * GROUP + local
                    flow[0, local, var, rows] = shifted_main(group, member, local, var, tile)
                    total = strip_part(total, group, member, local, var, local, tile)
                flow[0, GROUP, var, rows] = present(tile, total)

        @pl.loop(0, STEPS // 2 - 1)
        def _(pair):
            advance(0, 1, range(4))
            advance(1, 0, range(4))

        advance(0, 1, range(4))
        advance(1, 0, (1, 2))
        for local in range(GROUP):
            for var in range(3):
                for tile in range(2):
                    rows = pl.ds(16 + 8 * tile, 8)
                    main = roll(flow[0, local, var, rows], -WIDTH)
                    side = roll(flow[0, GROUP, var, rows], 128 - EDGE - local * STRIP)
                    at = pl.multiple_of((group * GROUP + local) * 48 + var * 16 + tile * 8, 8)
                    evolved[pl.ds(at, 8), :] = jnp.where(lane8 < 128 - 2 * WIDTH, main, side)

    flat = jnp.concatenate([evolved[pl.ds(j, 16, stride=48), :] for j in range(48)], axis=1)
    gram = lax.dot_general(
        flat,
        flat,
        (((1,), (1,)), ((), ())),
        precision=lax.Precision.HIGHEST,
        preferred_element_type=jnp.float32,
    )
    table[0:16, :] = jnp.zeros((16, 128), jnp.float32)
    table[0:16, 0:16] = gram
    row_id, lane = rows_of(16), lane16
    wide = table[0:16, :]
    wide = wide + roll(jnp.where((lane >= 8) & (lane < 12), wide, 0.0), 4)
    for shift in (16, 32, 64):
        wide = wide + roll(wide, shift)
    upper = (row_id < 8) & (lane // 16 == row_id) & (lane % 16 < 12)
    lower = (row_id >= 8) & (row_id < 12) & (lane // 16 == row_id - 8) & (lane % 16 >= 12)
    pick = upper | lower
    packed = jnp.sum(jnp.where(pick, wide, 0.0), axis=0, keepdims=True)

    def exchange(value, slot, buffer, me, count, peer_of, me_of, send, recv):
        row_out[slot] = value
        buffer[me] = value

        def copy(step, place):
            return pltpu.make_async_remote_copy(
                src_ref=row_out.at[slot],
                dst_ref=buffer.at[place],
                send_sem=send.at[step],
                recv_sem=recv.at[place],
                device_id=peer_of(step),
            )

        @pl.loop(1, count)
        def _(step):
            copy(step, me).start()

        @pl.loop(1, count)
        def _(step):
            copy(step, (me + step) % count).wait_recv()

        @pl.loop(1, count)
        def _(step):
            copy(step, me).wait_send()

        total = buffer[0]
        for index in range(1, count):
            total = total + buffer[index]
        return total

    packed = exchange(packed, 0, plane_in, me_plane, n_plane, plane_peer, None, plane_send, plane_recv)
    packed = exchange(packed, 1, column_in, level, n_level, column_peer, None, column_send, column_recv)

    cells = float(3 * 16 * n_lat * 128 * n_lon)
    work = jnp.broadcast_to(packed / cells, (16, 128))
    for bit in range(3):
        work = jnp.where((row_id // (1 << bit)) % 2 == 1, roll(work, -(16 << bit)), work)
    work = jnp.where(row_id >= 8, roll(work, -4), work)
    turned = jnp.transpose(work)[0:16, :]
    table[0:16, 0:16] = turned
    turned = table[0:16, :]
    work = jnp.where((row_id >= 8) & (lane < 8), turned, work)
    work = jnp.where((lane < 12) & (row_id < 12), work, 0.0)
    work = jnp.where((lane == row_id + 16) & (row_id < 12), 1.0, work)
    for k in range(MEMBERS - 1):
        pivot_row = work[k : k + 1, :]
        scaled = pivot_row / work[k : k + 1, k : k + 1]
        work = work - jnp.where(row_id > k, work[:, k : k + 1], 0.0) * scaled
    diagonal = jnp.sum(jnp.where(lane == row_id, work, 0.0), axis=1, keepdims=True)
    diagonal = jnp.where(row_id[:, 0:1] < MEMBERS, diagonal, 1.0)
    work = work / jnp.sqrt(diagonal)
    factor_ref[...] = jnp.where(lane >= row_id, work, 0.0)[0:MEMBERS, 0:MEMBERS]
    for k in range(MEMBERS):
        table[16 * k : 16 * k + 16, :] = jnp.broadcast_to(work[:, 16 + k : 17 + k], (16, 128))

    for var in range(3):
        for tile in range(2):
            inputs = [
                evolved[48 * m + 16 * var + 8 * tile : 48 * m + 16 * var + 8 * tile + 8, :]
                for m in range(MEMBERS)
            ]
            for m in range(MEMBERS):
                total = None
                for k in range(m + 1):
                    term = jnp.broadcast_to(table[16 * k + m : 16 * k + m + 1, :], (8, 128)) * inputs[k]
                    total = term if total is None else total + term
                fields_ref[m, var, 8 * tile : 8 * tile + 8, :] = total

    for piece in ("wind", "height", 0, 1, 2):
        for north in (True, False):
            when_sends(north, lambda: lat_copies(piece, north).wait_send())
    for to_east in (True, False):
        strip_copy(to_east, 0).wait_send()
        pl.when(has_north)(lambda: strip_copy(to_east, 1).wait_send())
        pl.when(has_south)(lambda: strip_copy(to_east, -1).wait_send())


def solution(mesh):
    n_lon, n_lat = mesh.shape["lon"], mesh.shape["lat"]
    n_plane, n_level = 2 * n_lat, n_lon // 2
    dma = pltpu.SemaphoreType.DMA

    def step(perturbations, base_wind, base_height):
        return pl.pallas_call(
            functools.partial(kernel, n_lon, n_lat),
            out_shape=(
                jax.ShapeDtypeStruct((MEMBERS, 3, 16, 128), jnp.float32),
                jax.ShapeDtypeStruct((MEMBERS, MEMBERS), jnp.float32),
            ),
            in_specs=[pl.BlockSpec(memory_space=pl.ANY)] * 3,
            out_specs=(pl.BlockSpec(memory_space=pltpu.VMEM), pl.BlockSpec(memory_space=pltpu.VMEM)),
            scratch_shapes=[
                pltpu.VMEM((MEMBERS + 1, 3, 32, 128), jnp.float32),
                pltpu.VMEM((GROUPS, 16, 128), jnp.float32),
                pltpu.VMEM((GROUPS, 16, 128), jnp.float32),
                pltpu.VMEM((GROUPS, 32, 128), jnp.float32),
                pltpu.VMEM((GROUPS, 32, 128), jnp.float32),
                pltpu.VMEM((2, GROUP + 1, 3, 48, 128), jnp.float32),
                pltpu.VMEM((2, 3, 48, 128), jnp.float32),
                pltpu.VMEM((COEFS, 2, 32, 128), jnp.float32),
                pltpu.VMEM((16 * 48, 128), jnp.float32),
                pltpu.VMEM((16 * MEMBERS, 128), jnp.float32),
                pltpu.VMEM((2, 1, 128), jnp.float32),
                pltpu.VMEM((n_plane, 1, 128), jnp.float32),
                pltpu.VMEM((n_level, 1, 128), jnp.float32),
                dma((3,)),
                dma((2, GROUPS + 2)),
                dma((2, GROUPS + 2)),
                dma((6,)),
                dma((6,)),
                dma((n_plane,)),
                dma((n_plane,)),
                dma((n_level,)),
                dma((n_level,)),
            ],
            compiler_params=pltpu.CompilerParams(collective_id=0, has_side_effects=True),
        )(perturbations, base_wind, base_height)

    return jax.shard_map(
        step,
        mesh=mesh,
        in_specs=(P(None, None, "lat", "lon"), P(None, "lat", "lon"), P("lat", "lon")),
        out_specs=(P(None, None, "lat", "lon"), P()),
        check_vma=False,
    )
```

time: 221 us -> 46.4 us (0.21)
  blocking collectives: 113 us -> 0 us
  starting transfers between devices: 57.2 us -> 0 us
  Pallas kernels: 0 us -> 43.4 us
  waiting for transfers between devices: 24.3 us -> 0 us
  other arithmetic: 19.3 us -> 0 us
    psum x1 -> x0, blocking collectives: 113 us -> none  [per_device(): gram = lax.psum(local_gram, ('lon', 'lat'))]
    ppermute x20 -> x0, starting transfers between devices: 57.2 us -> none  [the longest x10 32.8 us: with_halo(): lax.ppermute(lax.slice_in_dim(block, 0, width, axis=dim), axis, backward)]
    pallas_call x0 -> x1, Pallas kernels: none -> 43.4 us  [step(): pl.pallas_call(functools.partial(kernel, n_lon, n_lat), out_shape=(jax.Sh...]
    ppermute x20 -> x0, waiting for transfers between devices: 24.3 us -> none  [the longest x10 19.7 us: with_halo(): lax.ppermute(lax.slice_in_dim(block, 0, width, axis=dim), axis, backward)]
    another operation x32 -> x0, other arithmetic: 13.7 us -> none  [the longest x28 11 us: advance(): return jnp.stack([new_x, new_y, new_height], axis=-3)]
  transfers between devices with their start and end apart: 20 -> 0, of which waited for: 15 -> 0; matrix products, arithmetic and copies ran while one was open for 1% -> 0% of each run, Pallas kernels for 0% -> 0%
where the time goes in v1:
time: 46.4 us; the launch traced here: 46.3 us
  Pallas kernels  43.4 us (94%)
  local copies, waits for them, and re-layouts  2.3 us (5%)
  between operations  0.65 us (1%)
    pallas_call x1, Pallas kernels, step(): pl.pallas_call(functools.partial(kernel, n_lon, n_lat), out_shape=(jax.Sh...  43.4 us
    unnamed x4, local copies, waits for them, and re-layouts  2.3 us

profile of v1, /device:TPU:1, one launch (start us, length us, event | category | flops | bytes accessed | tf_op | source)
XLA Modules:
  0.0 46.3 jit_solution(12380873377895651613)
XLA Ops:
  0.6 43.4 %shard_map.50 = (f32[12,3,16,128]{3,2,1,0:T(8,128)}, f32[12,12]{1,0:T(8,128)}) custom-call(f32[12,3,16,128]{3,2,1,0:T(8,128)} %x_hbm.1, f32[2,16,128]{2,1,0:T(8,128)} %wind_hbm.1, f32[16,128]{1,0:T(8,128)} %height_hbm.1), custom_call_target="tpu_custom_call" | custom-call | tf_op jit(solution)/shard_map/pallas_call | solution.py:448
  44.0 0.0 copy-start
  44.0 1.7 %copy.7 = f32[12,3,16,128]{3,2,1,0:T(8,128)} copy(f32[12,3,16,128]{3,2,1,0:T(8,128)} %get-tuple-element.4) | data formatting | bytes 589824
  45.7 0.0 copy-done
  45.7 0.6 %copy.8 = f32[12,12]{1,0:T(8,128)} copy(f32[12,12]{1,0:T(8,128)S(1)} %copy-done) | data formatting | bytes 1152
Async XLA Ops:
  44.0 1.7 %copy-start = (f32[12,12]{1,0:T(8,128)S(1)}, f32[12,12]{1,0:T(8,128)}, u32[]{:S(2)}) copy-start(f32[12,12]{1,0:T(8,128)} %get-tuple-element.5) | copy-start | bytes 1732

commit v2 on v1

--- a/solution.py
+++ b/solution.py
@@ -24,7 +24,7 @@
 HALF = 0.5 * advect_rate
 KEEP = 1.0 - 4.0 * diffuse_rate
 PULL = 0.5 * gravity_rate
-COEFS = 13
+COEFS = 15
 
 
 def roll(value, shift):
@@ -41,7 +41,7 @@
 
 
 def slot_of(local, var):
-    return WIDTH * (3 * local + var)
+    return STRIP * local + WIDTH * var if local < GROUP else STRIP * var + EDGE
 
 
 def kernel(
@@ -65,6 +65,7 @@
     row_out,
     plane_in,
     column_in,
+    turns,
     load_sem,
     lat_send,
     lat_recv,
@@ -74,6 +75,8 @@
     plane_recv,
     column_send,
     column_recv,
+    plane_known,
+    level_known,
 ):
     lon = lax.axis_index("lon")
     lat = lax.axis_index("lat")
@@ -99,32 +102,42 @@
         load.start()
 
     def plane_peer(step):
-        index = (me_plane + step) % n_plane
-        return device(level * 2 + index % 2, index // 2)
+        index = me_plane ^ step
+        return device(level * 2 + (index & 1), index >> 1)
 
     def column_peer(step):
-        return device(((level + step) % n_level) * 2 + core, lat)
+        return device((level ^ step) * 2 + core, lat)
+
+    def level_peer(step):
+        return device(((level + step) & (n_level - 1)) * 2 + core, lat)
 
     barrier = pltpu.get_barrier_semaphore()
     across = jnp.where(core == 1, east, west)
-
-    @pl.loop(1, n_plane)
-    def _(step):
-        pl.semaphore_signal(barrier, inc=1, device_id=plane_peer(step))
-
-    @pl.loop(1, n_level)
-    def _(step):
-        pl.semaphore_signal(barrier, inc=1, device_id=column_peer(step))
-
-    pl.semaphore_signal(barrier, inc=1, device_id=device(across, lat))
-
-    @pl.when(has_south)
-    def _():
-        pl.semaphore_signal(barrier, inc=1, device_id=device(across, lat - 1))
-
-    @pl.when(has_north)
-    def _():
-        pl.semaphore_signal(barrier, inc=1, device_id=device(across, lat + 1))
+    mate = lon ^ 1
+    near = [plane_peer(step) for step in (1, 2, 3, 4, 5, 6, 7, 8, 16, 24)]
+    near += [level_peer(1), level_peer(-1), device(across, lat)]
+    for peer in near:
+        pl.semaphore_signal(barrier, inc=1, device_id=peer)
+    for there, row in ((has_south, lat - 1), (has_north, lat + 1)):
+
+        @pl.when(there)
+        def _():
+            for column in (lon, across, mate):
+                pl.semaphore_signal(barrier, inc=1, device_id=device(column, row))
+
+    for tile in range(4):
+        place = (lat * 16 - 8 + 8 * tile + rows_of(8)).astype(jnp.float32)
+        turns[8 * tile : 8 * tile + 8, :] = turn_rate * jnp.sin(math.pi * ((place + 0.5) / (16 * n_lat) - 0.5))
+    evolved[MEMBERS * 48 :, :] = jnp.zeros((4 * 48, 128), jnp.float32)
+    for parity in range(2):
+        for slot in range(GROUP + 1):
+            for var in range(3):
+                flow[parity, slot, var, 0:8] = jnp.zeros((8, 128), jnp.float32)
+                flow[parity, slot, var, 40:48] = jnp.zeros((8, 128), jnp.float32)
+    for kind in range(2):
+        for var in range(3):
+            base[kind, var, 0:8] = jnp.zeros((8, 128), jnp.float32)
+            base[kind, var, 40:48] = jnp.zeros((8, 128), jnp.float32)
 
     def lat_copies(piece, north):
         rows = pl.ds(8, 8) if north else pl.ds(0, 8)
@@ -189,8 +202,12 @@
 
     pl.semaphore_wait(
         barrier,
-        n_plane - 1 + n_level - 1 + 1 + has_south.astype(jnp.int32) + has_north.astype(jnp.int32),
+        len(near) + 3 * (has_south.astype(jnp.int32) + has_north.astype(jnp.int32)),
     )
+    for step in (8, 16, 24):
+        pl.semaphore_signal(plane_known, inc=1, device_id=plane_peer(step))
+    for step in (1, -1):
+        pl.semaphore_signal(level_known.at[0], inc=1, device_id=level_peer(step))
 
     for piece in ("wind", "height"):
         for north in (True, False):
@@ -203,16 +220,9 @@
         for north in (True, False):
             when_sends(north, lambda: lat_copies(piece, north).start())
 
-    evolved[MEMBERS * 48 :, :] = jnp.zeros((4 * 48, 128), jnp.float32)
-    for parity in range(2):
-        for slot in range(GROUP + 1):
-            for var in range(3):
-                flow[parity, slot, var, 0:8] = jnp.zeros((8, 128), jnp.float32)
-                flow[parity, slot, var, 40:48] = jnp.zeros((8, 128), jnp.float32)
-    for kind in range(2):
-        for var in range(3):
-            base[kind, var, 0:8] = jnp.zeros((8, 128), jnp.float32)
-            base[kind, var, 40:48] = jnp.zeros((8, 128), jnp.float32)
+    pl.semaphore_wait(level_known.at[0], 2)
+    for step in (2, -2):
+        pl.semaphore_signal(level_known.at[1], inc=1, device_id=level_peer(step))
 
     for piece in ("wind", "height"):
         for north in (True, False):
@@ -229,30 +239,31 @@
             return jnp.where(has_north, value, 0.0)
         return value
 
-    def shifted_main(group, member, local, var, tile):
-        rows = pl.ds(8 * tile, 8)
-        rim = roll(from_west[group, rows], -slot_of(local, var))
-        return present(tile, jnp.where(lane8 < WIDTH, rim, roll(ext[member, var, rows], WIDTH)))
-
-    def strip_part(total, group, member, local, var, place, tile):
-        rows = pl.ds(8 * tile, 8)
-        first = place * STRIP
-        own = roll(ext[member, var, rows], first - (128 - EDGE))
-        rim = roll(from_east[group, rows], first + EDGE - slot_of(local, var))
-        total = jnp.where((lane8 >= first) & (lane8 < first + EDGE), own, total)
-        return jnp.where((lane8 >= first + EDGE) & (lane8 < first + STRIP), rim, total)
+    def rows_at(tile):
+        return pl.ds(8 * tile, 8)
+
+    def main_part(group, member, local, var, tile):
+        rim = roll(from_west[group, rows_at(tile)], 128 - WIDTH - slot_of(local, var))
+        return present(tile, jnp.where(lane8 < 128 - WIDTH, ext[member, var, rows_at(tile)], rim))
+
+    def strip_own(total, member, var, place, tile):
+        own = roll(ext[member, var, rows_at(tile)], STRIP * place + WIDTH - (128 - EDGE))
+        return own if total is None else jnp.where((lane8 >= STRIP * place + WIDTH), own, total)
 
     for var in range(3):
         for tile in range(4):
             rows = pl.ds(8 + 8 * tile, 8)
-            base[0, var, rows] = shifted_main(0, MEMBERS, GROUP, var, tile)
-            total = jnp.zeros((8, 128), jnp.float32)
+            base[0, var, rows] = main_part(0, MEMBERS, GROUP, var, tile)
+            total = None
             for place in range(4):
-                total = strip_part(total, 0, MEMBERS, GROUP, var, place, tile)
+                total = strip_own(total, MEMBERS, var, place, tile)
+            for place in range(4):
+                rim = roll(from_east[0, rows_at(tile)], STRIP * (place + 1) - slot_of(GROUP, var))
+                first = STRIP * ((place + 1) % 4)
+                total = jnp.where((lane8 >= first) & (lane8 < first + WIDTH), rim, total)
             base[1, var, rows] = present(tile, total)
     for tile in range(4):
-        place = (lat * 16 - 8 + 8 * tile + rows_of(8)).astype(jnp.float32)
-        turning = jnp.sin(math.pi * ((place + 0.5) / (16 * n_lat) - 0.5))
+        turning = turns[8 * tile : 8 * tile + 8, :]
         for kind in range(2):
             here, up, down = pl.ds(8 + 8 * tile, 8), pl.ds(9 + 8 * tile, 8), pl.ds(7 + 8 * tile, 8)
             mean_x = base[kind, 0, here]
@@ -260,20 +271,23 @@
             depth = base[kind, 2, here]
             x_up, x_down = base[kind, 0, up], base[kind, 0, down]
             y_up, y_down = base[kind, 1, up], base[kind, 1, down]
+            x_east, x_west = roll(mean_x, -1), roll(mean_x, 1)
             values = [
+                diffuse_rate - HALF * x_west,
+                diffuse_rate + HALF * x_east,
                 diffuse_rate - HALF * mean_x,
                 diffuse_rate + HALF * mean_x,
-                diffuse_rate - HALF * mean_y,
-                diffuse_rate + HALF * mean_y,
-                KEEP - HALF * (roll(mean_x, -1) - roll(mean_x, 1)),
-                turn_rate * turning - HALF * (x_up - x_down),
+                present(tile, diffuse_rate - HALF * mean_y),
+                present(tile, diffuse_rate + HALF * mean_y),
+                KEEP - HALF * (x_east - x_west),
+                turning - HALF * (x_up - x_down),
                 KEEP - HALF * (y_up - y_down),
-                -turn_rate * turning - HALF * (roll(mean_y, -1) - roll(mean_y, 1)),
-                HALF * depth,
-                diffuse_rate - HALF * y_up,
-                diffuse_rate + HALF * y_down,
-                HALF * base[kind, 2, up],
-                HALF * base[kind, 2, down],
+                -turning - HALF * (roll(mean_y, -1) - roll(mean_y, 1)),
+                (PULL * HALF) * depth,
+                present(tile, diffuse_rate - HALF * y_up),
+                present(tile, diffuse_rate + HALF * y_down),
+                present(tile, (PULL * HALF) * base[kind, 2, up]),
+                present(tile, (PULL * HALF) * base[kind, 2, down]),
             ]
             for index, value in enumerate(values):
                 coef[index, kind, pl.ds(8 * tile, 8)] = value
@@ -282,35 +296,35 @@
         for tile in tiles:
             here, up, down = pl.ds(8 + 8 * tile, 8), pl.ds(9 + 8 * tile, 8), pl.ds(7 + 8 * tile, 8)
             for kind, slots in ((0, range(GROUP)), (1, (GROUP,))):
-                (e, w, n, s, keep_x, turn_x, keep_y, turn_y, deep, n_h, s_h, n_deep, s_deep) = [
-                    coef[index, kind, pl.ds(8 * tile, 8)] for index in range(COEFS)
+                (e, w, e_h, w_h, n, s, keep_x, turn_x, keep_y, turn_y, deep, n_h, s_h, n_deep, s_deep) = [
+                    coef[index, kind, rows_at(tile)] for index in range(COEFS)
                 ]
                 for slot in slots:
                     u, u_n, u_s = (flow[source, slot, 0, r] for r in (here, up, down))
                     v, v_n, v_s = (flow[source, slot, 1, r] for r in (here, up, down))
                     h, h_n, h_s = (flow[source, slot, 2, r] for r in (here, up, down))
-                    new_u = (
+                    carried = deep * u
+                    flow[target, slot, 0, here] = (
                         (keep_x * u + turn_x * v)
                         + (n * u_n + s * u_s)
-                        + (e * roll(u, -1) + w * roll(u, 1))
-                        - PULL * (roll(h, -1) - roll(h, 1))
+                        + (roll(e * u - h, -1) + roll(w * u + h, 1))
                     )
-                    new_v = (
+                    flow[target, slot, 1, here] = (
                         (keep_y * v + turn_y * u)
                         + (n * v_n + s * v_s)
-                        + (e * roll(v, -1) + w * roll(v, 1))
-                        - PULL * (h_n - h_s)
+                        + (roll(e * v, -1) + roll(w * v, 1))
+                        - present(tile, h_n - h_s)
                     )
-                    carried = deep * u
-                    new_h = (
+                    flow[target, slot, 2, here] = (
                         KEEP * h
-                        + (roll(e * h - carried, -1) + roll(w * h + carried, 1))
+                        + (roll(e_h * h - carried, -1) + roll(w_h * h + carried, 1))
                         + (n_h * h_n + s_h * h_s)
                         - (n_deep * v_n - s_deep * v_s)
                     )
-                    flow[target, slot, 0, here] = present(tile, new_u)
-                    flow[target, slot, 1, here] = present(tile, new_v)
-                    flow[target, slot, 2, here] = present(tile, new_h)
+
+    pl.semaphore_wait(level_known.at[1], 2)
+    for step in (4, -4):
+        pl.semaphore_signal(level_known.at[2], inc=1, device_id=level_peer(step))
 
     @pl.loop(0, GROUPS)
     def _(group):
@@ -319,12 +333,15 @@
         for var in range(3):
             for tile in range(4):
                 rows = pl.ds(8 + 8 * tile, 8)
-                total = jnp.zeros((8, 128), jnp.float32)
+                scale = PULL if var == 2 else 1.0
+                total = None
                 for local in range(GROUP):
                     member = group * GROUP + local
-                    flow[0, local, var, rows] = shifted_main(group, member, local, var, tile)
-                    total = strip_part(total, group, member, local, var, local, tile)
-                flow[0, GROUP, var, rows] = present(tile, total)
+                    flow[0, local, var, rows] = main_part(group, member, local, var, tile) * scale
+                    total = strip_own(total, member, var, local, tile)
+                rim = roll(from_east[group, rows_at(tile)], STRIP - WIDTH * var)
+                total = jnp.where(lane8 % STRIP < WIDTH, rim, total)
+                flow[0, GROUP, var, rows] = present(tile, total) * scale
 
         @pl.loop(0, STEPS // 2 - 1)
         def _(pair):
@@ -337,10 +354,12 @@
             for var in range(3):
                 for tile in range(2):
                     rows = pl.ds(16 + 8 * tile, 8)
-                    main = roll(flow[0, local, var, rows], -WIDTH)
-                    side = roll(flow[0, GROUP, var, rows], 128 - EDGE - local * STRIP)
+                    main = flow[0, local, var, rows]
+                    side = roll(flow[0, GROUP, var, rows], 128 - STRIP * (local + 1))
                     at = pl.multiple_of((group * GROUP + local) * 48 + var * 16 + tile * 8, 8)
-                    evolved[pl.ds(at, 8), :] = jnp.where(lane8 < 128 - 2 * WIDTH, main, side)
+                    evolved[pl.ds(at, 8), :] = (
+                        jnp.where(lane8 < 128 - 2 * WIDTH, main, side) * (1.0 / PULL if var == 2 else 1.0)
+                    )
 
     flat = jnp.concatenate([evolved[pl.ds(j, 16, stride=48), :] for j in range(48)], axis=1)
     gram = lax.dot_general(
@@ -362,38 +381,42 @@
     pick = upper | lower
     packed = jnp.sum(jnp.where(pick, wide, 0.0), axis=0, keepdims=True)
 
-    def exchange(value, slot, buffer, me, count, peer_of, me_of, send, recv):
+    def exchange_copy(slot, step, place):
+        buffer, peer_of, send, recv = (
+            (plane_in, plane_peer, plane_send, plane_recv),
+            (column_in, column_peer, column_send, column_recv),
+        )[slot]
+        return pltpu.make_async_remote_copy(
+            src_ref=row_out.at[slot],
+            dst_ref=buffer.at[place],
+            send_sem=send.at[step],
+            recv_sem=recv.at[place],
+            device_id=peer_of(step),
+        )
+
+    def exchange(value, slot, buffer, me, order):
         row_out[slot] = value
         buffer[me] = value
-
-        def copy(step, place):
-            return pltpu.make_async_remote_copy(
-                src_ref=row_out.at[slot],
-                dst_ref=buffer.at[place],
-                send_sem=send.at[step],
-                recv_sem=recv.at[place],
-                device_id=peer_of(step),
-            )
-
-        @pl.loop(1, count)
-        def _(step):
-            copy(step, me).start()
-
-        @pl.loop(1, count)
-        def _(step):
-            copy(step, (me + step) % count).wait_recv()
-
-        @pl.loop(1, count)
-        def _(step):
-            copy(step, me).wait_send()
-
-        total = buffer[0]
-        for index in range(1, count):
-            total = total + buffer[index]
-        return total
-
-    packed = exchange(packed, 0, plane_in, me_plane, n_plane, plane_peer, None, plane_send, plane_recv)
-    packed = exchange(packed, 1, column_in, level, n_level, column_peer, None, column_send, column_recv)
+        for step in order:
+            exchange_copy(slot, step, me).start()
+        for step in reversed(order):
+            exchange_copy(slot, step, me ^ step).wait_recv()
+        parts = [buffer[index] for index in range(len(order) + 1)]
+        while len(parts) > 1:
+            parts = [a + b for a, b in zip(parts[0::2], parts[1::2])]
+        return parts[0]
+
+    def hops(step):
+        pair = {0: 0, 1: 1, 2: 2, 3: 1}
+        return pair[(step >> 1) & 3] + pair[(step >> 3) & 3]
+
+    plane_order = sorted(range(1, n_plane), key=lambda step: -hops(step))
+    column_order = sorted(range(1, n_level), key=lambda step: -min(step, n_level - step))
+
+    pl.semaphore_wait(plane_known, 3)
+    packed = exchange(packed, 0, plane_in, me_plane, plane_order)
+    pl.semaphore_wait(level_known.at[2], 2)
+    packed = exchange(packed, 1, column_in, level, column_order)
 
     cells = float(3 * 16 * n_lat * 128 * n_lon)
     work = jnp.broadcast_to(packed / cells, (16, 128))
@@ -437,6 +460,10 @@
         strip_copy(to_east, 0).wait_send()
         pl.when(has_north)(lambda: strip_copy(to_east, 1).wait_send())
         pl.when(has_south)(lambda: strip_copy(to_east, -1).wait_send())
+    for step in plane_order:
+        exchange_copy(0, step, me_plane).wait_send()
+    for step in column_order:
+        exchange_copy(1, step, level).wait_send()
 
 
 def solution(mesh):
@@ -467,6 +494,7 @@
                 pltpu.VMEM((2, 1, 128), jnp.float32),
                 pltpu.VMEM((n_plane, 1, 128), jnp.float32),
                 pltpu.VMEM((n_level, 1, 128), jnp.float32),
+                pltpu.VMEM((32, 128), jnp.float32),
                 dma((3,)),
                 dma((2, GROUPS + 2)),
                 dma((2, GROUPS + 2)),
@@ -476,6 +504,8 @@
                 dma((n_plane,)),
                 dma((n_level,)),
                 dma((n_level,)),
+                pltpu.SemaphoreType.REGULAR,
+                pltpu.SemaphoreType.REGULAR((3,)),
             ],
             compiler_params=pltpu.CompilerParams(collective_id=0, has_side_effects=True),
         )(perturbations, base_wind, base_height)

time: 46.4 us -> 43 us (0.927)
  Pallas kernels: 43.4 us -> 39.9 us
    pallas_call x1, Pallas kernels: 43.4 us -> 39.9 us  [step(): pl.pallas_call(functools.partial(kernel, n_lon, n_lat), out_shape=(jax.Sh...]
where the time goes in v2:
time: 43 us; the launch traced here: 42.9 us
  Pallas kernels  39.9 us (93%)
  local copies, waits for them, and re-layouts  2.3 us (5%)
  between operations  0.65 us (2%)
    pallas_call x1, Pallas kernels, step(): pl.pallas_call(functools.partial(kernel, n_lon, n_lat), out_shape=(jax.Sh...  39.9 us
    unnamed x4, local copies, waits for them, and re-layouts  2.3 us

profile of v2, /device:TPU:1, one launch (start us, length us, event | category | flops | bytes accessed | tf_op | source)
XLA Modules:
  0.0 42.9 jit_solution(13339846998516061583)
XLA Ops:
  0.6 39.9 %shard_map.50 = (f32[12,3,16,128]{3,2,1,0:T(8,128)}, f32[12,12]{1,0:T(8,128)}) custom-call(f32[12,3,16,128]{3,2,1,0:T(8,128)} %x_hbm.1, f32[2,16,128]{2,1,0:T(8,128)} %wind_hbm.1, f32[16,128]{1,0:T(8,128)} %height_hbm.1), custom_call_target="tpu_custom_call" | custom-call | tf_op jit(solution)/shard_map/pallas_call | solution.py:475
  40.6 0.0 copy-start
  40.6 1.7 %copy.7 = f32[12,3,16,128]{3,2,1,0:T(8,128)} copy(f32[12,3,16,128]{3,2,1,0:T(8,128)} %get-tuple-element.4) | data formatting | bytes 589824
  42.3 0.0 copy-done
  42.3 0.6 %copy.8 = f32[12,12]{1,0:T(8,128)} copy(f32[12,12]{1,0:T(8,128)S(1)} %copy-done) | data formatting | bytes 1152
Async XLA Ops:
  40.6 1.7 %copy-start = (f32[12,12]{1,0:T(8,128)S(1)}, f32[12,12]{1,0:T(8,128)}, u32[]{:S(2)}) copy-start(f32[12,12]{1,0:T(8,128)} %get-tuple-element.5) | copy-start | bytes 1732

commit v3 on v2

--- a/solution.py
+++ b/solution.py
@@ -24,7 +24,7 @@
 HALF = 0.5 * advect_rate
 KEEP = 1.0 - 4.0 * diffuse_rate
 PULL = 0.5 * gravity_rate
-COEFS = 15
+COEFS = 16
 
 
 def roll(value, shift):
@@ -50,8 +50,8 @@
     x_hbm,
     wind_hbm,
     height_hbm,
-    fields_ref,
-    factor_ref,
+    evolved,
+    row_ref,
     ext,
     send_low,
     send_high,
@@ -60,7 +60,6 @@
     flow,
     base,
     coef,
-    evolved,
     table,
     row_out,
     plane_in,
@@ -181,6 +180,19 @@
 
     lane8 = lanes_of(8)
 
+    pl.semaphore_wait(
+        barrier,
+        len(near) + 3 * (has_south.astype(jnp.int32) + has_north.astype(jnp.int32)),
+    )
+    for step in (8, 16, 24):
+        pl.semaphore_signal(plane_known, inc=1, device_id=plane_peer(step))
+    for step in (1, -1):
+        pl.semaphore_signal(level_known.at[0], inc=1, device_id=level_peer(step))
+
+    for piece in ("wind", "height", 0):
+        for north in (True, False):
+            when_sends(north, lambda: lat_copies(piece, north).start())
+
     for load in loads:
         load.wait()
 
@@ -200,23 +212,11 @@
         send_low[group] = low
         send_high[group] = high
 
-    pl.semaphore_wait(
-        barrier,
-        len(near) + 3 * (has_south.astype(jnp.int32) + has_north.astype(jnp.int32)),
-    )
-    for step in (8, 16, 24):
-        pl.semaphore_signal(plane_known, inc=1, device_id=plane_peer(step))
-    for step in (1, -1):
-        pl.semaphore_signal(level_known.at[0], inc=1, device_id=level_peer(step))
-
-    for piece in ("wind", "height"):
-        for north in (True, False):
-            when_sends(north, lambda: lat_copies(piece, north).start())
     for to_east in (True, False):
-        strip_copy(to_east, 0).start()
         pl.when(has_north)(lambda: strip_copy(to_east, 1).start())
         pl.when(has_south)(lambda: strip_copy(to_east, -1).start())
-    for piece in range(GROUPS):
+        strip_copy(to_east, 0).start()
+    for piece in range(1, GROUPS):
         for north in (True, False):
             when_sends(north, lambda: lat_copies(piece, north).start())
 
@@ -288,17 +288,20 @@
                 present(tile, diffuse_rate + HALF * y_down),
                 present(tile, (PULL * HALF) * base[kind, 2, up]),
                 present(tile, (PULL * HALF) * base[kind, 2, down]),
+                present(tile, jnp.ones((8, 128), jnp.float32)),
             ]
             for index, value in enumerate(values):
                 coef[index, kind, pl.ds(8 * tile, 8)] = value
 
-    def advance(source, target, tiles):
-        for tile in tiles:
-            here, up, down = pl.ds(8 + 8 * tile, 8), pl.ds(9 + 8 * tile, 8), pl.ds(7 + 8 * tile, 8)
+    def advance(source, target, starts):
+        for start in starts:
+            here, up, down = pl.ds(8 + start, 8), pl.ds(9 + start, 8), pl.ds(7 + start, 8)
+            inner = 8 <= start <= 16
             for kind, slots in ((0, range(GROUP)), (1, (GROUP,))):
                 (e, w, e_h, w_h, n, s, keep_x, turn_x, keep_y, turn_y, deep, n_h, s_h, n_deep, s_deep) = [
-                    coef[index, kind, rows_at(tile)] for index in range(COEFS)
+                    coef[index, kind, pl.ds(start, 8)] for index in range(COEFS - 1)
                 ]
+                slope = None if inner else coef[COEFS - 1, kind, pl.ds(start, 8)]
                 for slot in slots:
                     u, u_n, u_s = (flow[source, slot, 0, r] for r in (here, up, down))
                     v, v_n, v_s = (flow[source, slot, 1, r] for r in (here, up, down))
@@ -313,7 +316,7 @@
                         (keep_y * v + turn_y * u)
                         + (n * v_n + s * v_s)
                         + (roll(e * v, -1) + roll(w * v, 1))
-                        - present(tile, h_n - h_s)
+                        - (h_n - h_s if inner else slope * (h_n - h_s))
                     )
                     flow[target, slot, 2, here] = (
                         KEEP * h
@@ -343,13 +346,9 @@
                 total = jnp.where(lane8 % STRIP < WIDTH, rim, total)
                 flow[0, GROUP, var, rows] = present(tile, total) * scale
 
-        @pl.loop(0, STEPS // 2 - 1)
-        def _(pair):
-            advance(0, 1, range(4))
-            advance(1, 0, range(4))
-
-        advance(0, 1, range(4))
-        advance(1, 0, (1, 2))
+        for index in range(STEPS):
+            starts = (0, 8, 16, 24) if index < 3 else (4, 12, 20) if index < 7 else (8, 16)
+            advance(index % 2, 1 - index % 2, starts)
         for local in range(GROUP):
             for var in range(3):
                 for tile in range(2):
@@ -394,11 +393,12 @@
             device_id=peer_of(step),
         )
 
-    def exchange(value, slot, buffer, me, order):
+    def exchange(value, slot, buffer, me, order, beside):
         row_out[slot] = value
         buffer[me] = value
         for step in order:
             exchange_copy(slot, step, me).start()
+        beside()
         for step in reversed(order):
             exchange_copy(slot, step, me ^ step).wait_recv()
         parts = [buffer[index] for index in range(len(order) + 1)]
@@ -406,6 +406,19 @@
             parts = [a + b for a, b in zip(parts[0::2], parts[1::2])]
         return parts[0]
 
+    def halo_sent():
+        for piece in ("wind", "height", 0, 1, 2):
+            for north in (True, False):
+                when_sends(north, lambda: lat_copies(piece, north).wait_send())
+        for to_east in (True, False):
+            strip_copy(to_east, 0).wait_send()
+            pl.when(has_north)(lambda: strip_copy(to_east, 1).wait_send())
+            pl.when(has_south)(lambda: strip_copy(to_east, -1).wait_send())
+
+    def plane_sent():
+        for step in plane_order:
+            exchange_copy(0, step, me_plane).wait_send()
+
     def hops(step):
         pair = {0: 0, 1: 1, 2: 2, 3: 1}
         return pair[(step >> 1) & 3] + pair[(step >> 3) & 3]
@@ -414,11 +427,19 @@
     column_order = sorted(range(1, n_level), key=lambda step: -min(step, n_level - step))
 
     pl.semaphore_wait(plane_known, 3)
-    packed = exchange(packed, 0, plane_in, me_plane, plane_order)
+    packed = exchange(packed, 0, plane_in, me_plane, plane_order, halo_sent)
     pl.semaphore_wait(level_known.at[2], 2)
-    packed = exchange(packed, 1, column_in, level, column_order)
-
-    cells = float(3 * 16 * n_lat * 128 * n_lon)
+    packed = exchange(packed, 1, column_in, level, column_order, plane_sent)
+
+    row_ref[...] = packed
+    for step in column_order:
+        exchange_copy(1, step, level).wait_send()
+
+
+def finish(cells, evolved, row_ref, fields_hbm, factor_ref, table, out, sems):
+    row_id, lane = rows_of(16), lanes_of(16)
+    packed = row_ref[...]
+
     work = jnp.broadcast_to(packed / cells, (16, 128))
     for bit in range(3):
         work = jnp.where((row_id // (1 << bit)) % 2 == 1, roll(work, -(16 << bit)), work)
@@ -440,30 +461,20 @@
     for k in range(MEMBERS):
         table[16 * k : 16 * k + 16, :] = jnp.broadcast_to(work[:, 16 + k : 17 + k], (16, 128))
 
-    for var in range(3):
-        for tile in range(2):
-            inputs = [
-                evolved[48 * m + 16 * var + 8 * tile : 48 * m + 16 * var + 8 * tile + 8, :]
-                for m in range(MEMBERS)
-            ]
-            for m in range(MEMBERS):
-                total = None
-                for k in range(m + 1):
-                    term = jnp.broadcast_to(table[16 * k + m : 16 * k + m + 1, :], (8, 128)) * inputs[k]
-                    total = term if total is None else total + term
-                fields_ref[m, var, 8 * tile : 8 * tile + 8, :] = total
-
-    for piece in ("wind", "height", 0, 1, 2):
-        for north in (True, False):
-            when_sends(north, lambda: lat_copies(piece, north).wait_send())
-    for to_east in (True, False):
-        strip_copy(to_east, 0).wait_send()
-        pl.when(has_north)(lambda: strip_copy(to_east, 1).wait_send())
-        pl.when(has_south)(lambda: strip_copy(to_east, -1).wait_send())
-    for step in plane_order:
-        exchange_copy(0, step, me_plane).wait_send()
-    for step in column_order:
-        exchange_copy(1, step, level).wait_send()
+    def copy_out(member):
+        return pltpu.make_async_copy(out.at[member], fields_hbm.at[member], sems.at[member])
+
+    for m in range(MEMBERS):
+        scale = [jnp.broadcast_to(table[16 * k + m : 16 * k + m + 1, :], (8, 128)) for k in range(m + 1)]
+        for place in range(6):
+            total = None
+            for k in range(m + 1):
+                term = scale[k] * evolved[48 * k + 8 * place : 48 * k + 8 * place + 8, :]
+                total = term if total is None else total + term
+            out[m, place // 2, 8 * (place % 2) : 8 * (place % 2) + 8, :] = total
+        copy_out(m).start()
+    for m in range(MEMBERS):
+        copy_out(m).wait()
 
 
 def solution(mesh):
@@ -472,11 +483,11 @@
     dma = pltpu.SemaphoreType.DMA
 
     def step(perturbations, base_wind, base_height):
-        return pl.pallas_call(
+        evolved, row = pl.pallas_call(
             functools.partial(kernel, n_lon, n_lat),
             out_shape=(
-                jax.ShapeDtypeStruct((MEMBERS, 3, 16, 128), jnp.float32),
-                jax.ShapeDtypeStruct((MEMBERS, MEMBERS), jnp.float32),
+                pltpu.VMEM((16 * 48, 128), jnp.float32),
+                pltpu.VMEM((1, 128), jnp.float32),
             ),
             in_specs=[pl.BlockSpec(memory_space=pl.ANY)] * 3,
             out_specs=(pl.BlockSpec(memory_space=pltpu.VMEM), pl.BlockSpec(memory_space=pltpu.VMEM)),
@@ -489,8 +500,7 @@
                 pltpu.VMEM((2, GROUP + 1, 3, 48, 128), jnp.float32),
                 pltpu.VMEM((2, 3, 48, 128), jnp.float32),
                 pltpu.VMEM((COEFS, 2, 32, 128), jnp.float32),
-                pltpu.VMEM((16 * 48, 128), jnp.float32),
-                pltpu.VMEM((16 * MEMBERS, 128), jnp.float32),
+                pltpu.VMEM((16, 128), jnp.float32),
                 pltpu.VMEM((2, 1, 128), jnp.float32),
                 pltpu.VMEM((n_plane, 1, 128), jnp.float32),
                 pltpu.VMEM((n_level, 1, 128), jnp.float32),
@@ -509,6 +519,23 @@
             ],
             compiler_params=pltpu.CompilerParams(collective_id=0, has_side_effects=True),
         )(perturbations, base_wind, base_height)
+        return pl.pallas_call(
+            functools.partial(finish, float(3 * 16 * n_lat * 128 * n_lon)),
+            out_shape=(
+                jax.ShapeDtypeStruct((MEMBERS, 3, 16, 128), jnp.float32),
+                jax.ShapeDtypeStruct((MEMBERS, MEMBERS), jnp.float32),
+            ),
+            in_specs=[pl.BlockSpec(memory_space=pltpu.VMEM)] * 2,
+            out_specs=(pl.BlockSpec(memory_space=pl.ANY), pl.BlockSpec(memory_space=pltpu.VMEM)),
+            scratch_shapes=[
+                pltpu.VMEM((16 * MEMBERS, 128), jnp.float32),
+                pltpu.VMEM((MEMBERS, 3, 16, 128), jnp.float32),
+                dma((MEMBERS,)),
+            ],
+        )(
+            pltpu.with_memory_space_constraint(evolved, pltpu.VMEM),
+            pltpu.with_memory_space_constraint(row, pltpu.VMEM),
+        )
 
     return jax.shard_map(
         step,

time: 43 us -> 40.5 us (0.942)
  local copies, waits for them, and re-layouts: 2.3 us -> 0 us
    unnamed x4 -> x0, local copies, waits for them, and re-layouts: 2.3 us -> none
    pallas_call x1 -> x2, Pallas kernels: 39.9 us -> 39.7 us  [the longest x1 37 us: step(): pl.pallas_call(functools.partial(kernel, n_lon, n_lat), out_shape=(pltpu....]
where the time goes in v3:
time: 40.5 us; the launch traced here: 40.4 us
  Pallas kernels  39.7 us (98%)
  between operations  0.64 us (2%)
    pallas_call x1, Pallas kernels, step(): pl.pallas_call(functools.partial(kernel, n_lon, n_lat), out_shape=(pltpu....  37 us
    pallas_call x1, Pallas kernels, step(): pl.pallas_call(functools.partial(finish, float(3 * 16 * n_lat * 128 * n_l...  2.75 us

profile of v3, /device:TPU:1, one launch (start us, length us, event | category | flops | bytes accessed | tf_op | source)
XLA Modules:
  0.0 40.4 jit_solution(11721970420418575549)
XLA Ops:
  0.6 37.0 %shard_map.50 = (f32[768,128]{1,0:T(8,128)S(1)}, f32[1,128]{1,0:T(1,128)S(1)}) custom-call(f32[12,3,16,128]{3,2,1,0:T(8,128)} %x_hbm.1, f32[2,16,128]{2,1,0:T(8,128)} %wind_hbm.1, f32[16,128]{1,0:T(8,128)} %height_hbm.1), custom_call_target="tpu_custom_call" | custom-call | tf_op jit(solution)/shard_map/pallas_call | solution.py:486
  37.6 2.7 %shard_map.51 = (f32[12,3,16,128]{3,2,1,0:T(8,128)}, f32[12,12]{1,0:T(8,128)}) custom-call(f32[768,128]{1,0:T(8,128)S(1)} %get-tuple-element.4.evolved, f32[1,128]{1,0:T(1,128)S(1)} %get-tuple-element.5.row_ref), custom_call_target="tpu_custom_call" | custom-call | tf_op jit(solution)/shard_map/pallas_call | solution.py:522

commit v4 on v3

--- a/solution.py
+++ b/solution.py
@@ -113,31 +113,22 @@
     barrier = pltpu.get_barrier_semaphore()
     across = jnp.where(core == 1, east, west)
     mate = lon ^ 1
-    near = [plane_peer(step) for step in (1, 2, 3, 4, 5, 6, 7, 8, 16, 24)]
-    near += [level_peer(1), level_peer(-1), device(across, lat)]
+    for there, row in ((has_south, lat - 1), (has_north, lat + 1)):
+
+        @pl.when(there)
+        def _():
+            for column in (across, mate, lon):
+                pl.semaphore_signal(barrier, inc=1, device_id=device(column, row))
+
+    near = [level_peer(step) for step in (3, -3, 2, -2, 1, -1)] + [device(across, lat)]
+    near += [plane_peer(step) for step in (16, 8, 24, 4, 5, 2, 3, 6, 7, 1)]
     for peer in near:
         pl.semaphore_signal(barrier, inc=1, device_id=peer)
-    for there, row in ((has_south, lat - 1), (has_north, lat + 1)):
-
-        @pl.when(there)
-        def _():
-            for column in (lon, across, mate):
-                pl.semaphore_signal(barrier, inc=1, device_id=device(column, row))
 
     for tile in range(4):
         place = (lat * 16 - 8 + 8 * tile + rows_of(8)).astype(jnp.float32)
         turns[8 * tile : 8 * tile + 8, :] = turn_rate * jnp.sin(math.pi * ((place + 0.5) / (16 * n_lat) - 0.5))
     evolved[MEMBERS * 48 :, :] = jnp.zeros((4 * 48, 128), jnp.float32)
-    for parity in range(2):
-        for slot in range(GROUP + 1):
-            for var in range(3):
-                flow[parity, slot, var, 0:8] = jnp.zeros((8, 128), jnp.float32)
-                flow[parity, slot, var, 40:48] = jnp.zeros((8, 128), jnp.float32)
-    for kind in range(2):
-        for var in range(3):
-            base[kind, var, 0:8] = jnp.zeros((8, 128), jnp.float32)
-            base[kind, var, 40:48] = jnp.zeros((8, 128), jnp.float32)
-
     def lat_copies(piece, north):
         rows = pl.ds(8, 8) if north else pl.ds(0, 8)
         place = pl.ds(0, 8) if north else pl.ds(24, 8)
@@ -180,19 +171,6 @@
 
     lane8 = lanes_of(8)
 
-    pl.semaphore_wait(
-        barrier,
-        len(near) + 3 * (has_south.astype(jnp.int32) + has_north.astype(jnp.int32)),
-    )
-    for step in (8, 16, 24):
-        pl.semaphore_signal(plane_known, inc=1, device_id=plane_peer(step))
-    for step in (1, -1):
-        pl.semaphore_signal(level_known.at[0], inc=1, device_id=level_peer(step))
-
-    for piece in ("wind", "height", 0):
-        for north in (True, False):
-            when_sends(north, lambda: lat_copies(piece, north).start())
-
     for load in loads:
         load.wait()
 
@@ -212,25 +190,26 @@
         send_low[group] = low
         send_high[group] = high
 
+    pl.semaphore_wait(
+        barrier,
+        len(near) + 3 * (has_south.astype(jnp.int32) + has_north.astype(jnp.int32)),
+    )
+    for step in (8, 16, 24):
+        pl.semaphore_signal(plane_known, inc=1, device_id=plane_peer(step))
+    for step in (3, -3):
+        pl.semaphore_signal(level_known.at[0], inc=1, device_id=level_peer(step))
+
+    for to_east in (True, False):
+        strip_copy(to_east, 0).start()
+    for piece in ("wind", "height"):
+        for north in (True, False):
+            when_sends(north, lambda: lat_copies(piece, north).start())
     for to_east in (True, False):
         pl.when(has_north)(lambda: strip_copy(to_east, 1).start())
         pl.when(has_south)(lambda: strip_copy(to_east, -1).start())
-        strip_copy(to_east, 0).start()
-    for piece in range(1, GROUPS):
+    for piece in range(GROUPS):
         for north in (True, False):
             when_sends(north, lambda: lat_copies(piece, north).start())
-
-    pl.semaphore_wait(level_known.at[0], 2)
-    for step in (2, -2):
-        pl.semaphore_signal(level_known.at[1], inc=1, device_id=level_peer(step))
-
-    for piece in ("wind", "height"):
-        for north in (True, False):
-            when_receives(north, lambda: lat_copies(piece, north).wait_recv())
-    for to_east in (True, False):
-        strip_copy(to_east, 0).wait_recv()
-        pl.when(has_south)(lambda: strip_copy(to_east, 1).wait_recv())
-        pl.when(has_north)(lambda: strip_copy(to_east, -1).wait_recv())
 
     def present(tile, value):
         if tile == 0:
@@ -250,22 +229,44 @@
         own = roll(ext[member, var, rows_at(tile)], STRIP * place + WIDTH - (128 - EDGE))
         return own if total is None else jnp.where((lane8 >= STRIP * place + WIDTH), own, total)
 
-    for var in range(3):
-        for tile in range(4):
-            rows = pl.ds(8 + 8 * tile, 8)
+    def inside(start, value):
+        row = rows_of(8) + start
+        if start < 8:
+            return jnp.where((row >= 8) | has_south, value, 0.0)
+        if start > 16:
+            return jnp.where((row < 24) | has_north, value, 0.0)
+        return value
+
+    def place_base(tile):
+        rows = rows_at(tile)
+        for var in range(3):
             base[0, var, rows] = main_part(0, MEMBERS, GROUP, var, tile)
             total = None
             for place in range(4):
                 total = strip_own(total, MEMBERS, var, place, tile)
             for place in range(4):
-                rim = roll(from_east[0, rows_at(tile)], STRIP * (place + 1) - slot_of(GROUP, var))
+                rim = roll(from_east[0, rows], STRIP * (place + 1) - slot_of(GROUP, var))
                 first = STRIP * ((place + 1) % 4)
                 total = jnp.where((lane8 >= first) & (lane8 < first + WIDTH), rim, total)
             base[1, var, rows] = present(tile, total)
-    for tile in range(4):
-        turning = turns[8 * tile : 8 * tile + 8, :]
+
+    def place_members(group, tile):
+        rows = rows_at(tile)
+        for var in range(3):
+            scale = PULL if var == 2 else 1.0
+            total = None
+            for local in range(GROUP):
+                member = group * GROUP + local
+                flow[group, 0, local, var, rows] = main_part(group, member, local, var, tile) * scale
+                total = strip_own(total, member, var, local, tile)
+            rim = roll(from_east[group, rows], STRIP - WIDTH * var)
+            total = jnp.where(lane8 % STRIP < WIDTH, rim, total)
+            flow[group, 0, GROUP, var, rows] = present(tile, total) * scale
+
+    def rates(start):
+        here, up, down = pl.ds(start, 8), pl.ds(start + 1, 8), pl.ds(start - 1, 8)
+        turning = turns[start : start + 8, :]
         for kind in range(2):
-            here, up, down = pl.ds(8 + 8 * tile, 8), pl.ds(9 + 8 * tile, 8), pl.ds(7 + 8 * tile, 8)
             mean_x = base[kind, 0, here]
             mean_y = base[kind, 1, here]
             depth = base[kind, 2, here]
@@ -277,25 +278,25 @@
                 diffuse_rate + HALF * x_east,
                 diffuse_rate - HALF * mean_x,
                 diffuse_rate + HALF * mean_x,
-                present(tile, diffuse_rate - HALF * mean_y),
-                present(tile, diffuse_rate + HALF * mean_y),
+                inside(start, diffuse_rate - HALF * mean_y),
+                inside(start, diffuse_rate + HALF * mean_y),
                 KEEP - HALF * (x_east - x_west),
                 turning - HALF * (x_up - x_down),
                 KEEP - HALF * (y_up - y_down),
                 -turning - HALF * (roll(mean_y, -1) - roll(mean_y, 1)),
                 (PULL * HALF) * depth,
-                present(tile, diffuse_rate - HALF * y_up),
-                present(tile, diffuse_rate + HALF * y_down),
-                present(tile, (PULL * HALF) * base[kind, 2, up]),
-                present(tile, (PULL * HALF) * base[kind, 2, down]),
-                present(tile, jnp.ones((8, 128), jnp.float32)),
+                inside(start, diffuse_rate - HALF * y_up),
+                inside(start, diffuse_rate + HALF * y_down),
+                inside(start, (PULL * HALF) * base[kind, 2, up]),
+                inside(start, (PULL * HALF) * base[kind, 2, down]),
+                inside(start, jnp.ones((8, 128), jnp.float32)),
             ]
             for index, value in enumerate(values):
-                coef[index, kind, pl.ds(8 * tile, 8)] = value
-
-    def advance(source, target, starts):
+                coef[index, kind, here] = value
+
+    def advance(group, source, target, starts):
         for start in starts:
-            here, up, down = pl.ds(8 + start, 8), pl.ds(9 + start, 8), pl.ds(7 + start, 8)
+            here, up, down = pl.ds(start, 8), pl.ds(start + 1, 8), pl.ds(start - 1, 8)
             inner = 8 <= start <= 16
             for kind, slots in ((0, range(GROUP)), (1, (GROUP,))):
                 (e, w, e_h, w_h, n, s, keep_x, turn_x, keep_y, turn_y, deep, n_h, s_h, n_deep, s_deep) = [
@@ -303,62 +304,77 @@
                 ]
                 slope = None if inner else coef[COEFS - 1, kind, pl.ds(start, 8)]
                 for slot in slots:
-                    u, u_n, u_s = (flow[source, slot, 0, r] for r in (here, up, down))
-                    v, v_n, v_s = (flow[source, slot, 1, r] for r in (here, up, down))
-                    h, h_n, h_s = (flow[source, slot, 2, r] for r in (here, up, down))
+                    u, u_n, u_s = (flow[group, source, slot, 0, r] for r in (here, up, down))
+                    v, v_n, v_s = (flow[group, source, slot, 1, r] for r in (here, up, down))
+                    h, h_n, h_s = (flow[group, source, slot, 2, r] for r in (here, up, down))
                     carried = deep * u
-                    flow[target, slot, 0, here] = (
+                    flow[group, target, slot, 0, here] = (
                         (keep_x * u + turn_x * v)
                         + (n * u_n + s * u_s)
                         + (roll(e * u - h, -1) + roll(w * u + h, 1))
                     )
-                    flow[target, slot, 1, here] = (
+                    flow[group, target, slot, 1, here] = (
                         (keep_y * v + turn_y * u)
                         + (n * v_n + s * v_s)
                         + (roll(e * v, -1) + roll(w * v, 1))
                         - (h_n - h_s if inner else slope * (h_n - h_s))
                     )
-                    flow[target, slot, 2, here] = (
+                    flow[group, target, slot, 2, here] = (
                         KEEP * h
                         + (roll(e_h * h - carried, -1) + roll(w_h * h + carried, 1))
                         + (n_h * h_n + s_h * h_s)
                         - (n_deep * v_n - s_deep * v_s)
                     )
 
-    pl.semaphore_wait(level_known.at[1], 2)
-    for step in (4, -4):
-        pl.semaphore_signal(level_known.at[2], inc=1, device_id=level_peer(step))
+    for to_east in (True, False):
+        strip_copy(to_east, 0).wait_recv()
+    for tile in (1, 2):
+        place_base(tile)
+    for start in (9, 15):
+        rates(start)
+
+    @pl.loop(0, GROUPS)
+    def _(group):
+        for tile in (1, 2):
+            place_members(group, tile)
+        for index, starts in enumerate(((9, 15), (10, 14), (11, 13), (12,))):
+            advance(group, index % 2, 1 - index % 2, starts)
+
+    for piece in ("wind", "height"):
+        for north in (True, False):
+            when_receives(north, lambda: lat_copies(piece, north).wait_recv())
+    for to_east in (True, False):
+        pl.when(has_south)(lambda: strip_copy(to_east, 1).wait_recv())
+        pl.when(has_north)(lambda: strip_copy(to_east, -1).wait_recv())
+    for tile in (0, 3):
+        place_base(tile)
+    for start in (1, 23):
+        rates(start)
 
     @pl.loop(0, GROUPS)
     def _(group):
         for north in (True, False):
             when_receives(north, lambda: lat_copies(group, north).wait_recv())
-        for var in range(3):
-            for tile in range(4):
-                rows = pl.ds(8 + 8 * tile, 8)
-                scale = PULL if var == 2 else 1.0
-                total = None
-                for local in range(GROUP):
-                    member = group * GROUP + local
-                    flow[0, local, var, rows] = main_part(group, member, local, var, tile) * scale
-                    total = strip_own(total, member, var, local, tile)
-                rim = roll(from_east[group, rows_at(tile)], STRIP - WIDTH * var)
-                total = jnp.where(lane8 % STRIP < WIDTH, rim, total)
-                flow[0, GROUP, var, rows] = present(tile, total) * scale
-
-        for index in range(STEPS):
-            starts = (0, 8, 16, 24) if index < 3 else (4, 12, 20) if index < 7 else (8, 16)
-            advance(index % 2, 1 - index % 2, starts)
+        for tile in (0, 3):
+            place_members(group, tile)
+
+        rest = ((1, 23), (2, 22), (3, 21), (4, 20), (5, 12, 19), (6, 12, 18), (7, 12, 17), (8, 16))
+        for index, starts in enumerate(rest):
+            advance(group, index % 2, 1 - index % 2, starts)
         for local in range(GROUP):
             for var in range(3):
                 for tile in range(2):
-                    rows = pl.ds(16 + 8 * tile, 8)
-                    main = flow[0, local, var, rows]
-                    side = roll(flow[0, GROUP, var, rows], 128 - STRIP * (local + 1))
+                    rows = pl.ds(8 + 8 * tile, 8)
+                    main = flow[group, 0, local, var, rows]
+                    side = roll(flow[group, 0, GROUP, var, rows], 128 - STRIP * (local + 1))
                     at = pl.multiple_of((group * GROUP + local) * 48 + var * 16 + tile * 8, 8)
                     evolved[pl.ds(at, 8), :] = (
                         jnp.where(lane8 < 128 - 2 * WIDTH, main, side) * (1.0 / PULL if var == 2 else 1.0)
                     )
+
+    pl.semaphore_wait(level_known.at[0], 2)
+    for step in (4, -4):
+        pl.semaphore_signal(level_known.at[1], inc=1, device_id=level_peer(step))
 
     flat = jnp.concatenate([evolved[pl.ds(j, 16, stride=48), :] for j in range(48)], axis=1)
     gram = lax.dot_general(
@@ -428,7 +444,7 @@
 
     pl.semaphore_wait(plane_known, 3)
     packed = exchange(packed, 0, plane_in, me_plane, plane_order, halo_sent)
-    pl.semaphore_wait(level_known.at[2], 2)
+    pl.semaphore_wait(level_known.at[1], 2)
     packed = exchange(packed, 1, column_in, level, column_order, plane_sent)
 
     row_ref[...] = packed
@@ -449,17 +465,28 @@
     turned = table[0:16, :]
     work = jnp.where((row_id >= 8) & (lane < 8), turned, work)
     work = jnp.where((lane < 12) & (row_id < 12), work, 0.0)
-    work = jnp.where((lane == row_id + 16) & (row_id < 12), 1.0, work)
-    for k in range(MEMBERS - 1):
-        pivot_row = work[k : k + 1, :]
-        scaled = pivot_row / work[k : k + 1, k : k + 1]
-        work = work - jnp.where(row_id > k, work[:, k : k + 1], 0.0) * scaled
-    diagonal = jnp.sum(jnp.where(lane == row_id, work, 0.0), axis=1, keepdims=True)
-    diagonal = jnp.where(row_id[:, 0:1] < MEMBERS, diagonal, 1.0)
-    work = work / jnp.sqrt(diagonal)
-    factor_ref[...] = jnp.where(lane >= row_id, work, 0.0)[0:MEMBERS, 0:MEMBERS]
+    left = [jnp.broadcast_to(work[:, k : k + 1], (16, 128)) for k in range(MEMBERS)]
+    right = [jnp.where(row_id == k, 1.0, 0.0) for k in range(MEMBERS)]
+    scales = []
     for k in range(MEMBERS):
-        table[16 * k : 16 * k + 16, :] = jnp.broadcast_to(work[:, 16 + k : 17 + k], (16, 128))
+        pivot = left[k][k : k + 1, :]
+        scales.append(pivot)
+        if k == MEMBERS - 1:
+            break
+        weight = jnp.where(row_id > k, left[k] * (1.0 / pivot), 0.0)
+        for j in range(k + 1, MEMBERS):
+            left[j] = left[j] - weight * left[j][k : k + 1, :]
+        for j in range(k + 1):
+            right[j] = right[j] - weight * right[j][k : k + 1, :]
+    spread = jnp.ones((16, 128), jnp.float32)
+    for k in range(MEMBERS):
+        spread = jnp.where(row_id == k, scales[k], spread)
+    spread = 1.0 / jnp.sqrt(spread)
+    factor = jnp.zeros((16, 128), jnp.float32)
+    for k in range(MEMBERS):
+        factor = jnp.where((lane == k) & (row_id <= k), left[k], factor)
+        table[16 * k : 16 * k + 16, :] = right[k] * spread
+    factor_ref[...] = (factor * spread)[0:MEMBERS, 0:MEMBERS]
 
     def copy_out(member):
         return pltpu.make_async_copy(out.at[member], fields_hbm.at[member], sems.at[member])
@@ -497,8 +524,8 @@
                 pltpu.VMEM((GROUPS, 16, 128), jnp.float32),
                 pltpu.VMEM((GROUPS, 32, 128), jnp.float32),
                 pltpu.VMEM((GROUPS, 32, 128), jnp.float32),
-                pltpu.VMEM((2, GROUP + 1, 3, 48, 128), jnp.float32),
-                pltpu.VMEM((2, 3, 48, 128), jnp.float32),
+                pltpu.VMEM((GROUPS, 2, GROUP + 1, 3, 32, 128), jnp.float32),
+                pltpu.VMEM((2, 3, 32, 128), jnp.float32),
                 pltpu.VMEM((COEFS, 2, 32, 128), jnp.float32),
                 pltpu.VMEM((16, 128), jnp.float32),
                 pltpu.VMEM((2, 1, 128), jnp.float32),
@@ -515,7 +542,7 @@
                 dma((n_level,)),
                 dma((n_level,)),
                 pltpu.SemaphoreType.REGULAR,
-                pltpu.SemaphoreType.REGULAR((3,)),
+                pltpu.SemaphoreType.REGULAR((2,)),
             ],
             compiler_params=pltpu.CompilerParams(collective_id=0, has_side_effects=True),
         )(perturbations, base_wind, base_height)

time: 40.5 us -> 39.6 us (0.978)
  Pallas kernels: 39.7 us -> 38.8 us
    pallas_call x1, Pallas kernels: 2.75 us -> 1.96 us  [step(): pl.pallas_call(functools.partial(finish, float(3 * 16 * n_lat * 128 * n_l...]
where the time goes in v4:
time: 39.6 us; the launch traced here: 39.4 us
  Pallas kernels  38.8 us (98%)
  between operations  0.64 us (2%)
    pallas_call x1, Pallas kernels, step(): pl.pallas_call(functools.partial(kernel, n_lon, n_lat), out_shape=(pltpu....  36.8 us
    pallas_call x1, Pallas kernels, step(): pl.pallas_call(functools.partial(finish, float(3 * 16 * n_lat * 128 * n_l...  1.96 us

profile of v4, /device:TPU:1, one launch (start us, length us, event | category | flops | bytes accessed | tf_op | source)
XLA Modules:
  0.0 39.4 jit_solution(9194453410871448065)
XLA Ops:
  0.6 36.8 %shard_map.50 = (f32[768,128]{1,0:T(8,128)S(1)}, f32[1,128]{1,0:T(1,128)S(1)}) custom-call(f32[12,3,16,128]{3,2,1,0:T(8,128)} %x_hbm.1, f32[2,16,128]{2,1,0:T(8,128)} %wind_hbm.1, f32[16,128]{1,0:T(8,128)} %height_hbm.1), custom_call_target="tpu_custom_call" | custom-call | tf_op jit(solution)/shard_map/pallas_call | solution.py:513
  37.5 2.0 %shard_map.51 = (f32[12,3,16,128]{3,2,1,0:T(8,128)}, f32[12,12]{1,0:T(8,128)}) custom-call(f32[768,128]{1,0:T(8,128)S(1)} %get-tuple-element.4.evolved, f32[1,128]{1,0:T(1,128)S(1)} %get-tuple-element.5.row_ref), custom_call_target="tpu_custom_call" | custom-call | tf_op jit(solution)/shard_map/pallas_call | solution.py:549

commit v5 on v4

--- a/solution.py
+++ b/solution.py
@@ -452,7 +452,7 @@
         exchange_copy(1, step, level).wait_send()
 
 
-def finish(cells, evolved, row_ref, fields_hbm, factor_ref, table, out, sems):
+def finish(cells, evolved, row_ref, fields_hbm, factor_hbm, table, out, factor_ref, sems):
     row_id, lane = rows_of(16), lanes_of(16)
     packed = row_ref[...]
 
@@ -487,6 +487,8 @@
         factor = jnp.where((lane == k) & (row_id <= k), left[k], factor)
         table[16 * k : 16 * k + 16, :] = right[k] * spread
     factor_ref[...] = (factor * spread)[0:MEMBERS, 0:MEMBERS]
+    factor_out = pltpu.make_async_copy(factor_ref, factor_hbm, sems.at[MEMBERS])
+    factor_out.start()
 
     def copy_out(member):
         return pltpu.make_async_copy(out.at[member], fields_hbm.at[member], sems.at[member])
@@ -500,6 +502,7 @@
                 total = term if total is None else total + term
             out[m, place // 2, 8 * (place % 2) : 8 * (place % 2) + 8, :] = total
         copy_out(m).start()
+    factor_out.wait()
     for m in range(MEMBERS):
         copy_out(m).wait()
 
@@ -553,11 +556,12 @@
                 jax.ShapeDtypeStruct((MEMBERS, MEMBERS), jnp.float32),
             ),
             in_specs=[pl.BlockSpec(memory_space=pltpu.VMEM)] * 2,
-            out_specs=(pl.BlockSpec(memory_space=pl.ANY), pl.BlockSpec(memory_space=pltpu.VMEM)),
+            out_specs=(pl.BlockSpec(memory_space=pl.ANY), pl.BlockSpec(memory_space=pl.ANY)),
             scratch_shapes=[
                 pltpu.VMEM((16 * MEMBERS, 128), jnp.float32),
                 pltpu.VMEM((MEMBERS, 3, 16, 128), jnp.float32),
-                dma((MEMBERS,)),
+                pltpu.VMEM((MEMBERS, MEMBERS), jnp.float32),
+                dma((MEMBERS + 1,)),
             ],
         )(
             pltpu.with_memory_space_constraint(evolved, pltpu.VMEM),

time: 39.6 us -> 39 us (0.985)
  Pallas kernels: 38.8 us -> 38.3 us
    pallas_call x1, Pallas kernels: 1.96 us -> 1.44 us  [step(): pl.pallas_call(functools.partial(finish, float(3 * 16 * n_lat * 128 * n_l...]
where the time goes in v5:
time: 39 us; the launch traced here: 38.9 us
  Pallas kernels  38.3 us (98%)
  between operations  0.64 us (2%)
    pallas_call x1, Pallas kernels, step(): pl.pallas_call(functools.partial(kernel, n_lon, n_lat), out_shape=(pltpu....  36.8 us
    pallas_call x1, Pallas kernels, step(): pl.pallas_call(functools.partial(finish, float(3 * 16 * n_lat * 128 * n_l...  1.44 us

profile of v5, /device:TPU:1, one launch (start us, length us, event | category | flops | bytes accessed | tf_op | source)
XLA Modules:
  0.0 38.9 jit_solution(3494653860522979014)
XLA Ops:
  0.6 36.8 %shard_map.50 = (f32[768,128]{1,0:T(8,128)S(1)}, f32[1,128]{1,0:T(1,128)S(1)}) custom-call(f32[12,3,16,128]{3,2,1,0:T(8,128)} %x_hbm.1, f32[2,16,128]{2,1,0:T(8,128)} %wind_hbm.1, f32[16,128]{1,0:T(8,128)} %height_hbm.1), custom_call_target="tpu_custom_call" | custom-call | tf_op jit(solution)/shard_map/pallas_call | solution.py:516
  37.5 1.4 %shard_map.51 = (f32[12,3,16,128]{3,2,1,0:T(8,128)}, f32[12,12]{1,0:T(8,128)}) custom-call(f32[768,128]{1,0:T(8,128)S(1)} %get-tuple-element.4.evolved, f32[1,128]{1,0:T(1,128)S(1)} %get-tuple-element.5.row_ref), custom_call_target="tpu_custom_call" | custom-call | tf_op jit(solution)/shard_map/pallas_call | solution.py:552

commit v6 on v5

--- a/solution.py
+++ b/solution.py
@@ -404,9 +404,19 @@
         return pltpu.make_async_remote_copy(
             src_ref=row_out.at[slot],
             dst_ref=buffer.at[place],
-            send_sem=send.at[step],
-            recv_sem=recv.at[place],
+            send_sem=send,
+            recv_sem=recv,
             device_id=peer_of(step),
+        )
+
+    def exchange_all(slot):
+        buffer, peer_of, send, recv = (
+            (plane_in, plane_peer, plane_send, plane_recv),
+            (column_in, column_peer, column_send, column_recv),
+        )[slot]
+        rows = buffer.at[pl.ds(1, buffer.shape[0] - 1)]
+        return pltpu.make_async_remote_copy(
+            src_ref=rows, dst_ref=rows, send_sem=send, recv_sem=recv, device_id=peer_of(1)
         )
 
     def exchange(value, slot, buffer, me, order, beside):
@@ -415,8 +425,7 @@
         for step in order:
             exchange_copy(slot, step, me).start()
         beside()
-        for step in reversed(order):
-            exchange_copy(slot, step, me ^ step).wait_recv()
+        exchange_all(slot).wait_recv()
         parts = [buffer[index] for index in range(len(order) + 1)]
         while len(parts) > 1:
             parts = [a + b for a, b in zip(parts[0::2], parts[1::2])]
@@ -432,8 +441,7 @@
             pl.when(has_south)(lambda: strip_copy(to_east, -1).wait_send())
 
     def plane_sent():
-        for step in plane_order:
-            exchange_copy(0, step, me_plane).wait_send()
+        exchange_all(0).wait_send()
 
     def hops(step):
         pair = {0: 0, 1: 1, 2: 2, 3: 1}
@@ -448,8 +456,7 @@
     packed = exchange(packed, 1, column_in, level, column_order, plane_sent)
 
     row_ref[...] = packed
-    for step in column_order:
-        exchange_copy(1, step, level).wait_send()
+    exchange_all(1).wait_send()
 
 
 def finish(cells, evolved, row_ref, fields_hbm, factor_hbm, table, out, factor_ref, sems):
@@ -540,10 +547,10 @@
                 dma((2, GROUPS + 2)),
                 dma((6,)),
                 dma((6,)),
-                dma((n_plane,)),
-                dma((n_plane,)),
-                dma((n_level,)),
-                dma((n_level,)),
+                dma,
+                dma,
+                dma,
+                dma,
                 pltpu.SemaphoreType.REGULAR,
                 pltpu.SemaphoreType.REGULAR((2,)),
             ],

time: 39 us -> 38.2 us (0.979)
  Pallas kernels: 38.3 us -> 37.4 us
    pallas_call x1, Pallas kernels: 36.8 us -> 36 us  [step(): pl.pallas_call(functools.partial(kernel, n_lon, n_lat), out_shape=(pltpu....]
where the time goes in v6:
time: 38.2 us; the launch traced here: 38 us
  Pallas kernels  37.4 us (98%)
  between operations  0.64 us (2%)
    pallas_call x1, Pallas kernels, step(): pl.pallas_call(functools.partial(kernel, n_lon, n_lat), out_shape=(pltpu....  36 us
    pallas_call x1, Pallas kernels, step(): pl.pallas_call(functools.partial(finish, float(3 * 16 * n_lat * 128 * n_l...  1.44 us

profile of v6, /device:TPU:1, one launch (start us, length us, event | category | flops | bytes accessed | tf_op | source)
XLA Modules:
  0.0 38.0 jit_solution(12314885744636392198)
XLA Ops:
  0.6 36.0 %shard_map.50 = (f32[768,128]{1,0:T(8,128)S(1)}, f32[1,128]{1,0:T(1,128)S(1)}) custom-call(f32[12,3,16,128]{3,2,1,0:T(8,128)} %x_hbm.1, f32[2,16,128]{2,1,0:T(8,128)} %wind_hbm.1, f32[16,128]{1,0:T(8,128)} %height_hbm.1), custom_call_target="tpu_custom_call" | custom-call | tf_op jit(solution)/shard_map/pallas_call | solution.py:523
  36.6 1.4 %shard_map.51 = (f32[12,3,16,128]{3,2,1,0:T(8,128)}, f32[12,12]{1,0:T(8,128)}) custom-call(f32[768,128]{1,0:T(8,128)S(1)} %get-tuple-element.4.evolved, f32[1,128]{1,0:T(1,128)S(1)} %get-tuple-element.5.row_ref), custom_call_target="tpu_custom_call" | custom-call | tf_op jit(solution)/shard_map/pallas_call | solution.py:559
